TPU v7x, 32 devices: a whole 2x2x4 slice. The times are simulated.
32 devices in a mesh: node: 4 (over y, x), feat: 4 (over z), tm: 2 (over core).
Axes of the slice: x: 2, y: 2, z: 4, core: 2. Of those that a mesh axis runs over, the one named last changes fastest.
Arguments:
- tensor: float32 [2, 16384, 4096], P('tm', 'node', 'feat'), may hold values from -6 to 6
- basis: float32 [16384, 128], P('node'), may hold values from -0.046875 to 0.046875
Outputs:
- gram: float32 [4096, 4096], P('feat', ('node', 'tm'))
All inputs are finite; a program needn't handle non-finite values.
Results may differ from a plain program's by a relative error of at most 0.000073.
Values sent between devices are 32-bit elements; how exact they have to be, the bound alone decides.
No kernel may reach another device: no remote copies, remote signals or barrier semaphores. Data moves between devices by JAX's collectives and lax.ppermute only.
A program may use at most 128 MiB of HBM per device.

v0:
```python
import jax
import jax.numpy as jnp
from jax import lax
from jax.sharding import PartitionSpec as P


def body(tensor, basis):
    local_data = tensor[0]
    partial_proj = lax.dot_general(
        basis,
        local_data,
        (((0,), (0,)), ((), ())),
        precision=lax.Precision.HIGHEST,
        preferred_element_type=jnp.float32,
    )
    scale = 1.0 / (basis.shape[1] * lax.axis_size("tm"))
    block_proj = lax.psum(partial_proj, "node")
    full_proj = lax.all_gather(block_proj, "feat", axis=1, tiled=True)
    width = full_proj.shape[1] // lax.axis_size("node")
    columns = lax.dynamic_slice_in_dim(full_proj, lax.axis_index("node") * width, width, 1)
    term = lax.dot_general(
        block_proj,
        columns,
        (((0,), (0,)), ((), ())),
        precision=lax.Precision.HIGHEST,
        preferred_element_type=jnp.float32,
    )
    result = lax.psum_scatter(term * scale, "tm", scatter_dimension=1, tiled=True)
    return result


def solution(mesh):
    in_specs = (P("tm", "node", "feat"), P("node", None))
    out_specs = P("feat", ("node", "tm"))
    return jax.shard_map(body, mesh=mesh, in_specs=in_specs, out_specs=out_specs, check_vma=False)
```

profile of v0, /device:TPU:0, one launch (start us, length us, event | category | flops | bytes accessed | tf_op | source)
XLA Modules:
  0.0 141.4 jit_solution(4735564744402768312)
XLA Ops:
  6.5 0.0 copy-start
  6.5 0.0 all-reduce.2.cloned.1.call-start
  6.5 1.6 %copy-done = f32[4096,128]{1,0:T(8,128)S(1)} copy-done((f32[4096,128]{1,0:T(8,128)S(1)}, f32[4096,128]{1,0:T(8,128)}, u32[]{:S(2)}) %copy-start) | copy-done | bytes 2097176
  8.1 13.5 %fusion = f32[128,1024]{1,0:T(8,128)} fusion(f32[4096,128]{1,0:T(8,128)S(1)} %copy-done, f32[1,4096,1024]{2,1,0:T(8,128)} %param.2), kind=kOutput, calls=%fused_computation | convolution fusion | flops 6442450944 | bytes 19398656 | tf_op jit(solution)/shard_map/dot_general | solution.py:9
  21.6 0.0 all-reduce.2.cloned.1.call-update
  21.6 0.0 all-gather.2.cloned.1.call-start
  21.7 48.1 %all-reduce.2.cloned.1.call-done = f32[128,1024]{1,0:T(8,128)} async-done(((f32[128,1024]{1,0:T(8,128)}), f32[128,1024]{1,0:T(8,128)}) %all-reduce.2.cloned.1.call-update) | async-done | bytes 524304 | tf_op jit(solution)/shard_map/psum | solution.py:17
  69.8 0.0 all-gather.2.cloned.1.call-update
  69.8 0.0 reduce-scatter.2.cloned.1.call-start
  69.9 47.5 %all-gather.2.cloned.1.call-done = f32[128,4096]{1,0:T(8,128)} async-done(((f32[128,1024]{1,0:T(8,128)}), f32[128,4096]{1,0:T(8,128)}) %all-gather.2.cloned.1.call-update) | async-done | bytes 2097168 | tf_op jit(solution)/shard_map/all_gather | solution.py:18
  117.3 6.6 %convolution_multiply_fusion = f32[1024,1024]{1,0:T(8,128)} fusion(f32[128,1024]{1,0:T(8,128)} %all-reduce.2.cloned.1.call-done, f32[128,4096]{1,0:T(8,128)} %all-gather.2.cloned.1.call-done, s32[]{:T(128)S(6)} %select_n.3), kind=kOutput, calls=%fused_computation.2 | convolution fusion | flops 1611661312 | bytes 5242884 | tf_op jit(solution)/shard_map/dot_general | solution.py:21
  124.0 0.0 reduce-scatter.2.cloned.1.call-update
  124.0 10.9 %reduce-scatter.2.cloned.1.call-done = f32[1024,512]{1,0:T(8,128)} async-done(((f32[1024,1024]{1,0:T(8,128)}), f32[1024,512]{1,0:T(8,128)}) %reduce-scatter.2.cloned.1.call-update) | async-done | bytes 2097168 | tf_op jit(solution)/shard_map/reduce_scatter | solution.py:28
Async XLA Ops:
  6.5 1.6 %copy-start = (f32[4096,128]{1,0:T(8,128)S(1)}, f32[4096,128]{1,0:T(8,128)}, u32[]{:S(2)}) copy-start(f32[4096,128]{1,0:T(8,128)} %param.3) | copy-start | bytes 6291460
  6.5 63.3 %all-reduce.2.cloned.1.call-start = ((), (), s32[]{:S(2)}) async-start(), calls=%async_computation.1 | async-start | bytes 1048576 | tf_op jit(solution)/shard_map/psum | solution.py:17
  21.6 95.7 %all-gather.2.cloned.1.call-start = ((), (), s32[]{:S(2)}) async-start(), calls=%async_computation.2 | async-start | bytes 2621440 | tf_op jit(solution)/shard_map/all_gather | solution.py:18
  69.8 65.1 %reduce-scatter.2.cloned.1.call-start = ((), (), s32[]{:S(2)}) async-start(), calls=%async_computation.3 | async-start | bytes 6291456 | tf_op jit(solution)/shard_map/reduce_scatter | solution.py:28
Sparse Core Ops, SparseCore 0:
  21.7 48.0 all-reduce.1
  71.4 45.9 all-gather.1
  124.1 10.7 reduce-scatter.1
where the time goes:
time: 142 us; the launch traced here: 141 us
  waiting for transfers between devices  107 us (75%)
  matrix products  20.1 us (14%)
  between operations  13.1 us (9%)
  local copies, waits for them, and re-layouts  1.59 us (1%)
    psum x1, waiting for transfers between devices, body(): block_proj = lax.psum(partial_proj, 'node')  48.1 us
    all_gather x1, waiting for transfers between devices, body(): full_proj = lax.all_gather(block_proj, 'feat', axis=1, tiled=True)  47.5 us
    dot_general x1, matrix products, body(): lax.dot_general(basis, local_data, (((0,), (0,)), ((), ())), precision=la...  13.5 us
    reduce_scatter x1, waiting for transfers between devices, body(): lax.psum_scatter(term * scale, 'tm', scatter_dimension=1, tiled=True)  10.9 us
    dot_general x1, matrix products, body(): lax.dot_general(block_proj, columns, (((0,), (0,)), ((), ())), precision=...  6.61 us
  transfers between devices with their start and end apart: 3, of which 3 were waited for; matrix products, arithmetic and copies ran while one was open for 0% of the time, Pallas kernels for 0%

commit v1 on v0

v1 whole, which is shorter than its diff:
```python
import jax
import jax.numpy as jnp
from jax import lax
from jax.sharding import PartitionSpec as P

TM_SWAP = [(0, 1), (1, 0)]


def body(tensor, basis):
    nodes = lax.axis_size("node")
    feats = lax.axis_size("feat")
    times = lax.axis_size("tm")
    rank = basis.shape[1]
    width = tensor.shape[2]
    groups = nodes // feats
    rows = rank // nodes
    cols = width // (groups * times)
    scale = 1.0 / (rank * times)

    partial = lax.dot_general(
        basis,
        tensor[0],
        (((0,), (0,)), ((), ())),
        precision=lax.Precision.HIGH,
        preferred_element_type=jnp.float32,
    )

    pieces = partial.reshape(nodes, rows, groups, times, cols).transpose(0, 3, 1, 2, 4)
    pieces = pieces.reshape(nodes * times, rows, groups * cols)
    pieces = lax.all_to_all(pieces, ("node", "tm"), 0, 0, tiled=True)
    share = jnp.sum(pieces.reshape(nodes, times * rows, groups * cols), axis=0)

    blocks = lax.all_gather(share, "feat", axis=0, tiled=False)
    right = blocks.reshape(feats, times * rows, groups, cols).transpose(0, 2, 1, 3)
    right = right.reshape(nodes, times * rows, cols)
    left = jnp.broadcast_to(share[None], (nodes, times * rows, groups * cols))
    both = lax.all_to_all(jnp.concatenate([left, right], axis=2), "node", 0, 0, tiled=True)
    depth = nodes * times * rows
    left = both[:, :, : groups * cols].reshape(depth, groups * cols)
    right = both[:, :, groups * cols :].reshape(depth, cols)

    other = lax.ppermute(left, "tm", TM_SWAP)
    core = lax.axis_index("tm")
    even = jnp.where(core == 0, left, other).reshape(depth, groups, 1, cols)
    odd = jnp.where(core == 0, other, left).reshape(depth, groups, 1, cols)
    full = jnp.concatenate([even, odd], axis=2).reshape(depth, width)
    gram = lax.dot_general(
        full,
        right,
        (((0,), (0,)), ((), ())),
        precision=lax.Precision.HIGH,
        preferred_element_type=jnp.float32,
    )
    return gram * scale


def solution(mesh):
    in_specs = (P("tm", "node", "feat"), P("node", None))
    out_specs = P("feat", ("node", "tm"))
    return jax.shard_map(body, mesh=mesh, in_specs=in_specs, out_specs=out_specs, check_vma=False)
```

time: 142 us -> 82 us (0.58)
  waiting for transfers between devices: 107 us -> 1.89 us
  blocking collectives: 0 us -> 45 us
  local copies, waits for them, and re-layouts: 1.59 us -> 19.9 us
  between operations: 13.1 us -> 0.08 us
  matrix products: 20.1 us -> 14.2 us
    psum x1 -> x0, waiting for transfers between devices: 48.1 us -> none  [body(): block_proj = lax.psum(partial_proj, 'node')]
    all_gather x1 -> x0, waiting for transfers between devices: 47.5 us -> none  [body(): full_proj = lax.all_gather(block_proj, 'feat', axis=1, tiled=True)]
    all_to_all x0 -> x2, blocking collectives: none -> 29.6 us  [the longest x1 14.9 us: body(): lax.all_to_all(jnp.concatenate([left, right], axis=2), 'node', 0, 0, tile...]
    another operation x0 -> x1, local copies, waits for them, and re-layouts: none -> 17.5 us
    all_gather x0 -> x1, blocking collectives: none -> 15.4 us  [body(): blocks = lax.all_gather(share, 'feat', axis=0, tiled=False)]
    reduce_scatter x1 -> x0, waiting for transfers between devices: 10.9 us -> none  [body(): lax.psum_scatter(term * scale, 'tm', scatter_dimension=1, tiled=True)]
    dot_general x2, matrix products: 20.1 us -> 14.2 us  [the longest x1 11.9 us: body(): lax.dot_general(basis, tensor[0], (((0,), (0,)), ((), ())), precision=lax...]
    ppermute x0 -> x1, waiting for transfers between devices: none -> 1.89 us  [body(): other = lax.ppermute(left, 'tm', TM_SWAP)]
  transfers between devices with their start and end apart: 3 -> 1, of which waited for: 3 -> 1; matrix products, arithmetic and copies ran while one was open for 0% -> 0% of each run, Pallas kernels for 0% -> 0%
where the time goes in v1:
time: 82 us; the launch traced here: 81.5 us
  blocking collectives  45 us (55%)
  local copies, waits for them, and re-layouts  19.9 us (24%)
  matrix products  14.2 us (17%)
  waiting for transfers between devices  1.89 us (2%)
    another operation x1, local copies, waits for them, and re-layouts  17.5 us
    all_gather x1, blocking collectives, body(): blocks = lax.all_gather(share, 'feat', axis=0, tiled=False)  15.4 us
    all_to_all x1, blocking collectives, body(): lax.all_to_all(jnp.concatenate([left, right], axis=2), 'node', 0, 0, tile...  14.9 us
    all_to_all x1, blocking collectives, body(): pieces = lax.all_to_all(pieces, ('node', 'tm'), 0, 0, tiled=True)  14.7 us
    dot_general x1, matrix products, body(): lax.dot_general(basis, tensor[0], (((0,), (0,)), ((), ())), precision=lax...  11.9 us
    dot_general x1, matrix products, body(): lax.dot_general(full, right, (((0,), (0,)), ((), ())), precision=lax.Prec...  2.32 us
    unnamed x1, local copies, waits for them, and re-layouts  1.92 us
    ppermute x1, waiting for transfers between devices, body(): other = lax.ppermute(left, 'tm', TM_SWAP)  1.89 us
  transfers between devices with their start and end apart: 1, of which 1 were waited for; matrix products, arithmetic and copies ran while one was open for 0% of the time, Pallas kernels for 0%

profile of v1, /device:TPU:0, one launch (start us, length us, event | category | flops | bytes accessed | tf_op | source)
XLA Modules:
  0.0 81.5 jit_solution(9171353638103746167)
XLA Ops:
  0.0 17.5 %copy.11 = f32[1024,4096]{1,0:T(8,128)} copy(f32[1024,4096]{0,1:T(8,128)} %bitcast.36) | data formatting | bytes 33554432 | tf_op jit(solution)/shard_map/reshape.2
  17.5 1.9 %copy.7 = f32[4096,128]{0,1:T(8,128)S(1)} copy(f32[4096,128]{1,0:T(8,128)} %param.3) | data formatting | bytes 4194304 | tf_op args[1]
  19.4 11.9 %fusion.1 = f32[4,32,2,512]{3,1,2,0:T(8,128)S(1)} fusion(f32[4,32,4096,1]{2,1,3,0:T(8,128)S(1)} %bitcast.37, f32[2,512,4096,1]{2,1,0,3:T(8,128)} %bitcast.35), kind=kOutput, calls=%fused_computation.7 | convolution fusion | flops 3221225472 | bytes 19398656 | tf_op jit(solution)/shard_map/dot_general | solution.py:20
  31.4 14.7 %all_to_all.10 = f32[8,32,512]{2,1,0:T(8,128)S(1)} all-to-all(f32[8,32,512]{2,1,0:T(8,128)S(1)} %bitcast.39), channel_id=1, replica_groups=mesh['node'=4,'feat'=4,'tm'=2] {'node','tm'}, dimensions={0} | all-to-all | bytes 1048576 | tf_op jit(solution)/shard_map/all_to_all | solution.py:30
  46.1 15.4 %all-gather = f32[256,512]{1,0:T(8,128)S(1)} all-gather(f32[64,512]{1,0:T(8,128)S(1)} %bitcast_reduce_fusion), channel_id=2, replica_groups=mesh['node'=4,'feat'=4,'tm'=2] {'feat'}, dimensions={0}, use_global_device_ids=true | all-gather | bytes 655360 | tf_op jit(solution)/shard_map/all_gather | solution.py:33
  61.5 0.1 broadcast_in_dim.8
  61.6 0.1 pad_maximum_fusion
  61.7 14.9 %all_to_all.11 = f32[4,64,1024]{2,1,0:T(8,128)S(1)} all-to-all(f32[4,64,1024]{2,1,0:T(8,128)S(1)} %pad_maximum_fusion), channel_id=1, replica_groups=mesh['node'=4,'feat'=4,'tm'=2] {'node'}, dimensions={0} | all-to-all | bytes 2097152 | tf_op jit(solution)/shard_map/all_to_all | solution.py:37
  76.6 0.1 fusion
  76.7 0.1 collective-permute-start
  76.8 1.9 %collective-permute-done = f32[256,512]{1,0:T(8,128)S(1)} collective-permute-done((f32[256,512]{1,0:T(8,128)S(1)}, f32[256,512]{1,0:T(8,128)S(1)}, u32[]{:S(2)}, u32[]{:S(2)}) %collective-permute-start) | collective-permute-done | bytes 524320 | tf_op jit(solution)/shard_map/ppermute | solution.py:42
  78.6 0.1 select_bitcast_fusion.1
  78.8 0.1 pad_maximum_fusion.1
  78.9 0.3 copy.9
  79.2 2.3 %convolution_multiply_fusion = f32[1024,512]{1,0:T(8,128)} fusion(f32[256,1024]{0,1:T(8,128)S(1)} %bitcast.38, f32[256,512]{1,0:T(8,128)S(1)} %bitcast.41), kind=kOutput, calls=%fused_computation | convolution fusion | flops 805830656 | bytes 3670016 | tf_op jit(solution)/shard_map/dot_general | solution.py:47
  (1 shorter events, 0.0 us)
Async XLA Ops:
  76.7 2.0 %collective-permute-start = (f32[256,512]{1,0:T(8,128)S(1)}, f32[256,512]{1,0:T(8,128)S(1)}, u32[]{:S(2)}, u32[]{:S(2)}) collective-permute-start(f32[256,512]{1,0:T(8,128)S(1)} %bitcast.42), channel_id=1, source_target_pairs={{0,1},{1,0},{2,3},{3,2},{4,5},{5,4},{6,7},{7,6},{8,9},{9,8},{10,11... | collective-permute-start | bytes 1572872 | tf_op jit(solution)/shard_map/ppermute | solution.py:42

commit v2 on v0

v2 whole, which is shorter than its diff:
```python
import functools

import jax
import jax.numpy as jnp
from jax import lax
from jax.experimental import pallas as pl
from jax.experimental.pallas import tpu as pltpu
from jax.sharding import PartitionSpec as P

VMEM_LIMIT = 48 * 1024 * 1024


def split(x):
    high = x.astype(jnp.bfloat16)
    return high, (x - high.astype(jnp.float32)).astype(jnp.bfloat16)


def project_kernel(cols, chunk, basis_hbm, tensor_hbm, out, basis, tensor, factor, total, basis_sem, tensor_sem):
    depth, width = tensor.shape
    rank = basis.shape[1]
    nodes, cores, rows, _ = out.shape
    count = depth // chunk

    def basis_copy(k):
        part = pl.ds(k * chunk, chunk)
        return pltpu.make_async_copy(basis_hbm.at[part], basis.at[part], basis_sem.at[k])

    def tensor_copy(k):
        part = pl.ds(k * chunk, chunk)
        return pltpu.make_async_copy(tensor_hbm.at[0, part], tensor.at[part], tensor_sem.at[k])

    for k in range(count):
        basis_copy(k).start()
        tensor_copy(k).start()
    for k in range(count):
        part = slice(k * chunk, (k + 1) * chunk)
        basis_copy(k).wait()
        high, low = split(basis[part].T)
        factor[:rank, part] = high
        factor[rank:, part] = low
        tensor_copy(k).wait()
        high, low = split(tensor[part])
        first = jnp.dot(factor[:, part], high, preferred_element_type=jnp.float32)
        second = jnp.dot(factor[:rank, part], low, preferred_element_type=jnp.float32)
        term = first[:rank] + first[rank:] + second
        if k == 0:
            total[...] = term
        else:
            total[...] += term
    for g in range(width // (cores * cols)):
        for c in range(cores):
            start = (g * cores + c) * cols
            value = total[:, start : start + cols]
            out[:, c, :, g * cols : (g + 1) * cols] = value.reshape(nodes, rows, cols)


def project(tensor, basis, nodes, cores, groups, cols):
    _, depth, width = tensor.shape
    rank = basis.shape[1]
    chunk = depth // 8
    return pl.pallas_call(
        functools.partial(project_kernel, cols, chunk),
        in_specs=[pl.BlockSpec(memory_space=pl.ANY)] * 2,
        out_specs=pl.BlockSpec(memory_space=pltpu.VMEM),
        out_shape=jax.ShapeDtypeStruct((nodes, cores, rank // nodes, groups * cols), jnp.float32),
        scratch_shapes=[
            pltpu.VMEM((depth, rank), jnp.float32),
            pltpu.VMEM((depth, width), jnp.float32),
            pltpu.VMEM((2 * rank, depth), jnp.bfloat16),
            pltpu.VMEM((rank, width), jnp.float32),
            pltpu.SemaphoreType.DMA((8,)),
            pltpu.SemaphoreType.DMA((8,)),
        ],
        compiler_params=pltpu.CompilerParams(vmem_limit_bytes=VMEM_LIMIT),
        cost_estimate=pl.CostEstimate(
            flops=6 * rank * depth * width, bytes_accessed=4 * depth * (width + rank), transcendentals=0
        ),
        name="project",
    )(basis, tensor)


def gram_kernel(nodes, groups, cols, scale, place, *refs):
    own, other, come = refs[:nodes], refs[nodes : 2 * nodes], refs[2 * nodes : 3 * nodes]
    out, high_scr, low_scr = refs[3 * nodes :]
    rows = own[0].shape[0]
    step = pl.program_id(0)
    local = place[2] == 1

    @pl.when((step == 0) & local)
    def _():
        part = pl.ds(pl.multiple_of(place[1] * cols, cols), cols)
        for d in range(nodes):
            high, low = split(own[d][:, part])
            high_scr[d * rows : (d + 1) * rows] = high
            low_scr[d * rows : (d + 1) * rows] = low

    @pl.when((step == 0) & jnp.logical_not(local))
    def _():
        for p in range(nodes):
            high, low = split(come[p][...])
            part = pl.ds(pl.multiple_of(place[3 + p] * rows, rows), rows)
            high_scr[part] = high
            low_scr[part] = low

    def product(left, g):
        value = jnp.concatenate([ref[:, g * cols : (g + 1) * cols] for ref in left], axis=0)
        high, low = split(value.T)
        term = jnp.dot(high, high_scr[...], preferred_element_type=jnp.float32)
        term += jnp.dot(low, high_scr[...], preferred_element_type=jnp.float32)
        term += jnp.dot(high, low_scr[...], preferred_element_type=jnp.float32)
        out[...] = term * scale

    for g in range(groups):
        for side, left in enumerate((own, other)):
            pl.when(step == g * 2 + side)(functools.partial(product, left, g))


def gram_block(place, own, other, come, groups, cols, scale):
    nodes = len(own)
    rows, width = own[0].shape
    depth = nodes * rows
    whole = lambda shape: pl.BlockSpec(shape, lambda s, place: (0, 0))
    core_first = lambda s, place: ((s // 2) * 2 + (place[0] + s % 2) % 2, 0)
    return pl.pallas_call(
        functools.partial(gram_kernel, nodes, groups, cols, scale),
        grid_spec=pltpu.PrefetchScalarGridSpec(
            num_scalar_prefetch=1,
            grid=(2 * groups,),
            in_specs=[whole((rows, width))] * (2 * nodes) + [whole((rows, cols))] * nodes,
            out_specs=pl.BlockSpec((cols, cols), core_first),
            scratch_shapes=[pltpu.VMEM((depth, cols), jnp.bfloat16)] * 2,
        ),
        out_shape=jax.ShapeDtypeStruct((2 * width, cols), jnp.float32),
        compiler_params=pltpu.CompilerParams(vmem_limit_bytes=VMEM_LIMIT),
        cost_estimate=pl.CostEstimate(
            flops=12 * depth * width * cols, bytes_accessed=8 * width * cols, transcendentals=0
        ),
        name="gram",
    )(place, *own, *other, *come)


def body(tensor, basis):
    nodes, feats, cores = lax.axis_size("node"), lax.axis_size("feat"), lax.axis_size("tm")
    rank = basis.shape[1]
    width = tensor.shape[2]
    groups = nodes // feats
    rows = rank // nodes
    cols = width // (groups * cores)
    scale = 1.0 / (rank * cores)
    node, feat, core = lax.axis_index("node"), lax.axis_index("feat"), lax.axis_index("tm")

    pieces = project(tensor, basis, nodes, cores, groups, cols)
    pieces = pieces.reshape(nodes * cores, rows, groups * cols)
    pieces = lax.all_to_all(pieces, ("node", "tm"), 0, 0, tiled=True)
    share = jnp.sum(pieces.reshape(nodes, cores * rows, groups * cols), axis=0)

    own = [share]
    for d in range(1, nodes):
        own.append(lax.ppermute(share, "node", [(n, n ^ d) for n in range(nodes)]))

    targets = (feats - 1) * groups
    come = []
    for p in range(nodes):
        pairs = []
        for z in range(feats):
            for idx in range(targets):
                source = (z * groups) ^ ((p + idx) % nodes)
                d, g = idx // groups + 1, idx % groups
                pairs.append((source * feats + z, (z * groups + g) * feats + (z ^ d)))
        if groups == 1:
            part = share
        else:
            g = ((node ^ (feat * groups)) - p) % nodes % groups
            part = lax.dynamic_slice_in_dim(share, g * cols, cols, 1)
        come.append(lax.ppermute(part, ("node", "feat"), pairs))

    other = [lax.ppermute(x, "tm", [(0, 1), (1, 0)]) for x in own]
    block, g = node // groups, node % groups
    idx = ((feat ^ block) - 1) * groups + g
    slots = [(((p + idx) % nodes) ^ (block * groups)) ^ node for p in range(nodes)]
    place = jnp.stack([core, g, (block == feat).astype(jnp.int32), *slots]).astype(jnp.int32)
    return gram_block(place, own, other, come, groups, cols, scale)


def solution(mesh):
    in_specs = (P("tm", "node", "feat"), P("node", None))
    out_specs = P("feat", ("node", "tm"))
    return jax.shard_map(body, mesh=mesh, in_specs=in_specs, out_specs=out_specs, check_vma=False)
```

time: 142 us -> 49.9 us (0.35)
  the two profiles are of different devices: /device:TPU:0 before, /device:TPU:13 now
where the time goes in v2:
time: 49.9 us; the launch traced here: 49.7 us
  starting transfers between devices  20 us (40%)
  blocking collectives  11.7 us (23%)
  Pallas kernels  9.69 us (19%)
  waiting for transfers between devices  6.51 us (13%)
  local copies, waits for them, and re-layouts  1.67 us (3%)
    all_to_all x1, blocking collectives, body(): pieces = lax.all_to_all(pieces, ('node', 'tm'), 0, 0, tiled=True)  11.7 us
    ppermute x4, starting transfers between devices, body(): come.append(lax.ppermute(part, ('node', 'feat'), pairs))  11.4 us
    pallas_call x1, Pallas kernels, project(): pl.pallas_call(functools.partial(project_kernel, cols, chunk), in_specs=[...  6.73 us
    ppermute x4, starting transfers between devices, body(): other = [lax.ppermute(x, 'tm', [(0, 1), (1, 0)]) for x in own]  5.92 us
    pallas_call x1, Pallas kernels, gram_block(): pl.pallas_call(functools.partial(gram_kernel, nodes, groups, cols, scale)...  2.97 us
    ppermute x3, starting transfers between devices, body(): own.append(lax.ppermute(share, 'node', [(n, n ^ d) for n in range(nodes)]))  2.71 us
    ppermute x3, waiting for transfers between devices, body(): own.append(lax.ppermute(share, 'node', [(n, n ^ d) for n in range(nodes)]))  2.7 us
    ppermute x4, waiting for transfers between devices, body(): come.append(lax.ppermute(part, ('node', 'feat'), pairs))  2.56 us
  transfers between devices with their start and end apart: 11, of which 5 were waited for; matrix products, arithmetic and copies ran while one was open for 0% of the time, Pallas kernels for 0%

profile of v2, /device:TPU:13, one launch (start us, length us, event | category | flops | bytes accessed | tf_op | source)
XLA Modules:
  0.0 49.7 jit_solution(15739302166458046541)
XLA Ops:
  0.0 0.0 copy-start
  0.0 1.6 %copy-done = f32[4096,128]{1,0:T(8,128)S(1)} copy-done((f32[4096,128]{1,0:T(8,128)S(1)}, f32[4096,128]{1,0:T(8,128)}, u32[]{:S(2)}) %copy-start) | copy-done | bytes 2097176
  1.6 6.7 %project.1 = f32[4,2,32,512]{3,2,1,0:T(8,128)S(1)} custom-call(f32[4096,128]{1,0:T(8,128)S(1)} %copy-done, f32[1,4096,1024]{2,1,0:T(8,128)} %tensor_hbm.1), custom_call_target="tpu_custom_call" | custom-call | flops 3221225472 | bytes 18874368 | tf_op jit(solution)/shard_map/project/pallas_call | solution.py:61
  8.3 11.7 %all_to_all.5 = f32[8,32,512]{2,1,0:T(8,128)S(1)} all-to-all(f32[8,32,512]{2,1,0:T(8,128)S(1)} %bitcast.10), channel_id=1, replica_groups=mesh['node'=4,'feat'=4,'tm'=2] {'node','tm'}, dimensions={0} | all-to-all | bytes 1048576 | tf_op jit(solution)/shard_map/all_to_all | solution.py:154
  20.0 3.7 %collective-permute-start.10 = (f32[64,512]{1,0:T(8,128)S(1)}, f32[64,512]{1,0:T(8,128)S(1)}, u32[]{:S(2)}, u32[]{:S(2)}) collective-permute-start(f32[64,512]{1,0:T(8,128)S(1)} %bitcast_reduce_fusion.refs_0_), channel_id=1, source_target_pairs={{24,2},{0,4},{8,6},{18,8},{10,14},{2,12},{12,22},{20,16},{28,18},{... | collective-permute-start | bytes 393224 | tf_op jit(solution)/shard_map/ppermute | solution.py:175
  23.7 3.4 %collective-permute-start.9 = (f32[64,512]{1,0:T(8,128)S(1)}, f32[64,512]{1,0:T(8,128)S(1)}, u32[]{:S(2)}, u32[]{:S(2)}) collective-permute-start(f32[64,512]{1,0:T(8,128)S(1)} %bitcast_reduce_fusion.refs_0_), channel_id=1, source_target_pairs={{16,2},{24,4},{0,6},{26,8},{18,14},{10,12},{4,22},{12,16},{20,18},... | collective-permute-start | bytes 393224 | tf_op jit(solution)/shard_map/ppermute | solution.py:175
  27.2 3.0 %collective-permute-start.8 = (f32[64,512]{1,0:T(8,128)S(1)}, f32[64,512]{1,0:T(8,128)S(1)}, u32[]{:S(2)}, u32[]{:S(2)}) collective-permute-start(f32[64,512]{1,0:T(8,128)S(1)} %bitcast_reduce_fusion.refs_0_), channel_id=1, source_target_pairs={{8,2},{16,4},{24,6},{2,8},{26,14},{18,12},{28,22},{4,16},{12,18},{... | collective-permute-start | bytes 393224 | tf_op jit(solution)/shard_map/ppermute | solution.py:175
  30.2 0.1 collective-permute-start.2
  30.3 2.4 %collective-permute-start.1 = (f32[64,512]{1,0:T(8,128)S(1)}, f32[64,512]{1,0:T(8,128)S(1)}, u32[]{:S(2)}, u32[]{:S(2)}) collective-permute-start(f32[64,512]{1,0:T(8,128)S(1)} %bitcast_reduce_fusion.refs_0_), channel_id=1, source_target_pairs={{0,16},{8,24},{16,0},{24,8},{1,17},{9,25},{17,1},{25,9},{2,18},{10... | collective-permute-start | bytes 393224 | tf_op jit(solution)/shard_map/ppermute | solution.py:159
  32.6 0.0 collective-permute-done.10.refs_11_
  32.6 0.3 collective-permute-start
  32.9 0.0 collective-permute-done.9.refs_10_
  32.9 1.3 %collective-permute-start.7 = (f32[64,512]{1,0:T(8,128)S(1)}, f32[64,512]{1,0:T(8,128)S(1)}, u32[]{:S(2)}, u32[]{:S(2)}) collective-permute-start(f32[64,512]{1,0:T(8,128)S(1)} %bitcast_reduce_fusion.refs_0_), channel_id=1, source_target_pairs={{0,2},{8,4},{16,6},{10,8},{2,14},{26,12},{20,22},{28,16},{4,18},{3... | collective-permute-start | bytes 393224 | tf_op jit(solution)/shard_map/ppermute | solution.py:175
  34.2 2.6 %collective-permute-done.8.refs_9_ = f32[64,512]{1,0:T(8,128)S(1)} collective-permute-done((f32[64,512]{1,0:T(8,128)S(1)}, f32[64,512]{1,0:T(8,128)S(1)}, u32[]{:S(2)}, u32[]{:S(2)}) %collective-permute-start.8) | collective-permute-done | bytes 131104 | tf_op jit(solution)/shard_map/ppermute | solution.py:175
  36.7 3.3 %collective-permute-start.3 = (f32[64,512]{1,0:T(8,128)S(1)}, f32[64,512]{1,0:T(8,128)S(1)}, u32[]{:S(2)}, u32[]{:S(2)}) collective-permute-start(f32[64,512]{1,0:T(8,128)S(1)} %bitcast_reduce_fusion.refs_0_), channel_id=1, source_target_pairs={{0,1},{1,0},{2,3},{3,2},{4,5},{5,4},{6,7},{7,6},{8,9},{9,8},{10,11... | collective-permute-start | bytes 393224 | tf_op jit(solution)/shard_map/ppermute | solution.py:177
  40.1 0.4 collective-permute-done.2.refs_3_
  40.4 1.0 %collective-permute-start.6 = (f32[64,512]{1,0:T(8,128)S(1)}, f32[64,512]{1,0:T(8,128)S(1)}, u32[]{:S(2)}, u32[]{:S(2)}) collective-permute-start(f32[64,512]{1,0:T(8,128)S(1)} %collective-permute-done.2.refs_3_), channel_id=1, source_target_pairs={{0,1},{1,0},{2,3},{3,2},{4,5},{5,4},{6,7},{7,6},{8,9},{9,8},{10,11... | collective-permute-start | bytes 393224 | tf_op jit(solution)/shard_map/ppermute | solution.py:177
  41.4 2.3 %collective-permute-done.1.refs_2_ = f32[64,512]{1,0:T(8,128)S(1)} collective-permute-done((f32[64,512]{1,0:T(8,128)S(1)}, f32[64,512]{1,0:T(8,128)S(1)}, u32[]{:S(2)}, u32[]{:S(2)}) %collective-permute-start.1) | collective-permute-done | bytes 131104 | tf_op jit(solution)/shard_map/ppermute | solution.py:159
  43.8 1.6 %collective-permute-start.5 = (f32[64,512]{1,0:T(8,128)S(1)}, f32[64,512]{1,0:T(8,128)S(1)}, u32[]{:S(2)}, u32[]{:S(2)}) collective-permute-start(f32[64,512]{1,0:T(8,128)S(1)} %collective-permute-done.1.refs_2_), channel_id=1, source_target_pairs={{0,1},{1,0},{2,3},{3,2},{4,5},{5,4},{6,7},{7,6},{8,9},{9,8},{10,11... | collective-permute-start | bytes 393224 | tf_op jit(solution)/shard_map/ppermute | solution.py:177
  45.4 0.0 collective-permute-done.refs_1_
  45.4 0.0 collective-permute-start.4
  45.4 0.1 stack.32.place
  45.4 0.0 collective-permute-done.7.refs_8_
  45.4 0.0 collective-permute-done.3.refs_4_
  45.5 0.0 collective-permute-done.6.refs_7_
  45.5 0.9 %collective-permute-done.5.refs_6_ = f32[64,512]{1,0:T(8,128)S(1)} collective-permute-done((f32[64,512]{1,0:T(8,128)S(1)}, f32[64,512]{1,0:T(8,128)S(1)}, u32[]{:S(2)}, u32[]{:S(2)}) %collective-permute-start.5) | collective-permute-done | bytes 131104 | tf_op jit(solution)/shard_map/ppermute | solution.py:177
  46.3 0.4 collective-permute-done.4.refs_5_
  46.7 3.0 %gram.1 = f32[1024,512]{1,0:T(8,128)} custom-call(s32[7]{0:T(128)S(1)} %stack.32.place, f32[64,512]{1,0:T(8,128)S(1)} %bitcast_reduce_fusion.refs_0_, f32[64,512]{1,0:T(8,128)S(1)} %collective-permute-done.refs_1_, f32[64,512]{1,0:T(8,128)S(1)} %collective-permute-done.1.refs_2_, f32[64,512]{1,0:T(8,128)S(1)} %collective-permute-done.2.refs_3_, ...), custom_call_target="tpu_custom_call" | custom-call | flops 805306368 | bytes 2097152 | tf_op jit(solution)/shard_map/gram/pallas_call | solution.py:124
  (1 shorter events, 0.0 us)
Async XLA Ops:
  0.0 1.6 %copy-start = (f32[4096,128]{1,0:T(8,128)S(1)}, f32[4096,128]{1,0:T(8,128)}, u32[]{:S(2)}) copy-start(f32[4096,128]{1,0:T(8,128)} %basis_hbm.1) | copy-start | bytes 6291460
  20.0 12.6 %collective-permute-start.10 = (f32[64,512]{1,0:T(8,128)S(1)}, f32[64,512]{1,0:T(8,128)S(1)}, u32[]{:S(2)}, u32[]{:S(2)}) collective-permute-start(f32[64,512]{1,0:T(8,128)S(1)} %bitcast_reduce_fusion.refs_0_), channel_id=1, source_target_pairs={{24,2},{0,4},{8,6},{18,8},{10,14},{2,12},{12,22},{20,16},{28,18},{... | collective-permute-start | bytes 393224 | tf_op jit(solution)/shard_map/ppermute | solution.py:175
  23.7 9.1 %collective-permute-start.9 = (f32[64,512]{1,0:T(8,128)S(1)}, f32[64,512]{1,0:T(8,128)S(1)}, u32[]{:S(2)}, u32[]{:S(2)}) collective-permute-start(f32[64,512]{1,0:T(8,128)S(1)} %bitcast_reduce_fusion.refs_0_), channel_id=1, source_target_pairs={{16,2},{24,4},{0,6},{26,8},{18,14},{10,12},{4,22},{12,16},{20,18},... | collective-permute-start | bytes 393224 | tf_op jit(solution)/shard_map/ppermute | solution.py:175
  27.2 9.5 %collective-permute-start.8 = (f32[64,512]{1,0:T(8,128)S(1)}, f32[64,512]{1,0:T(8,128)S(1)}, u32[]{:S(2)}, u32[]{:S(2)}) collective-permute-start(f32[64,512]{1,0:T(8,128)S(1)} %bitcast_reduce_fusion.refs_0_), channel_id=1, source_target_pairs={{8,2},{16,4},{24,6},{2,8},{26,14},{18,12},{28,22},{4,16},{12,18},{... | collective-permute-start | bytes 393224 | tf_op jit(solution)/shard_map/ppermute | solution.py:175
  30.2 10.3 %collective-permute-start.2 = (f32[64,512]{1,0:T(8,128)S(1)}, f32[64,512]{1,0:T(8,128)S(1)}, u32[]{:S(2)}, u32[]{:S(2)}) collective-permute-start(f32[64,512]{1,0:T(8,128)S(1)} %bitcast_reduce_fusion.refs_0_), channel_id=1, source_target_pairs={{0,24},{8,16},{16,8},{24,0},{1,25},{9,17},{17,9},{25,1},{2,26},{10... | collective-permute-start | bytes 393224 | tf_op jit(solution)/shard_map/ppermute | solution.py:159
  30.3 13.5 %collective-permute-start.1 = (f32[64,512]{1,0:T(8,128)S(1)}, f32[64,512]{1,0:T(8,128)S(1)}, u32[]{:S(2)}, u32[]{:S(2)}) collective-permute-start(f32[64,512]{1,0:T(8,128)S(1)} %bitcast_reduce_fusion.refs_0_), channel_id=1, source_target_pairs={{0,16},{8,24},{16,0},{24,8},{1,17},{9,25},{17,1},{25,9},{2,18},{10... | collective-permute-start | bytes 393224 | tf_op jit(solution)/shard_map/ppermute | solution.py:159
  32.6 12.7 %collective-permute-start = (f32[64,512]{1,0:T(8,128)S(1)}, f32[64,512]{1,0:T(8,128)S(1)}, u32[]{:S(2)}, u32[]{:S(2)}) collective-permute-start(f32[64,512]{1,0:T(8,128)S(1)} %bitcast_reduce_fusion.refs_0_), channel_id=1, source_target_pairs={{0,8},{8,0},{16,24},{24,16},{1,9},{9,1},{17,25},{25,17},{2,10},{10... | collective-permute-start | bytes 393224 | tf_op jit(solution)/shard_map/ppermute | solution.py:159
  32.9 12.6 %collective-permute-start.7 = (f32[64,512]{1,0:T(8,128)S(1)}, f32[64,512]{1,0:T(8,128)S(1)}, u32[]{:S(2)}, u32[]{:S(2)}) collective-permute-start(f32[64,512]{1,0:T(8,128)S(1)} %bitcast_reduce_fusion.refs_0_), channel_id=1, source_target_pairs={{0,2},{8,4},{16,6},{10,8},{2,14},{26,12},{20,22},{28,16},{4,18},{3... | collective-permute-start | bytes 393224 | tf_op jit(solution)/shard_map/ppermute | solution.py:175
  36.7 8.7 %collective-permute-start.3 = (f32[64,512]{1,0:T(8,128)S(1)}, f32[64,512]{1,0:T(8,128)S(1)}, u32[]{:S(2)}, u32[]{:S(2)}) collective-permute-start(f32[64,512]{1,0:T(8,128)S(1)} %bitcast_reduce_fusion.refs_0_), channel_id=1, source_target_pairs={{0,1},{1,0},{2,3},{3,2},{4,5},{5,4},{6,7},{7,6},{8,9},{9,8},{10,11... | collective-permute-start | bytes 393224 | tf_op jit(solution)/shard_map/ppermute | solution.py:177
  40.4 5.0 %collective-permute-start.6 = (f32[64,512]{1,0:T(8,128)S(1)}, f32[64,512]{1,0:T(8,128)S(1)}, u32[]{:S(2)}, u32[]{:S(2)}) collective-permute-start(f32[64,512]{1,0:T(8,128)S(1)} %collective-permute-done.2.refs_3_), channel_id=1, source_target_pairs={{0,1},{1,0},{2,3},{3,2},{4,5},{5,4},{6,7},{7,6},{8,9},{9,8},{10,11... | collective-permute-start | bytes 393224 | tf_op jit(solution)/shard_map/ppermute | solution.py:177
  43.8 2.6 %collective-permute-start.5 = (f32[64,512]{1,0:T(8,128)S(1)}, f32[64,512]{1,0:T(8,128)S(1)}, u32[]{:S(2)}, u32[]{:S(2)}) collective-permute-start(f32[64,512]{1,0:T(8,128)S(1)} %collective-permute-done.1.refs_2_), channel_id=1, source_target_pairs={{0,1},{1,0},{2,3},{3,2},{4,5},{5,4},{6,7},{7,6},{8,9},{9,8},{10,11... | collective-permute-start | bytes 393224 | tf_op jit(solution)/shard_map/ppermute | solution.py:177
  45.4 1.3 %collective-permute-start.4 = (f32[64,512]{1,0:T(8,128)S(1)}, f32[64,512]{1,0:T(8,128)S(1)}, u32[]{:S(2)}, u32[]{:S(2)}) collective-permute-start(f32[64,512]{1,0:T(8,128)S(1)} %collective-permute-done.refs_1_), channel_id=1, source_target_pairs={{0,1},{1,0},{2,3},{3,2},{4,5},{5,4},{6,7},{7,6},{8,9},{9,8},{10,11... | collective-permute-start | bytes 393224 | tf_op jit(solution)/shard_map/ppermute | solution.py:177

commit v3 on v2

v3 whole, which is shorter than its diff:
```python
import functools

import jax
import jax.numpy as jnp
from jax import lax
from jax.experimental import pallas as pl
from jax.experimental.pallas import tpu as pltpu
from jax.sharding import PartitionSpec as P

VMEM_LIMIT = 56 * 1024 * 1024


def split(x):
    high = x.astype(jnp.bfloat16)
    return high, (x - high.astype(jnp.float32)).astype(jnp.bfloat16)


def project_kernel(chunk, basis_hbm, tensor_hbm, out, basis, tensor, factor, total, basis_sem, tensor_sem):
    depth, width = tensor.shape
    rank = basis.shape[1]
    nodes, rows, _ = out.shape
    count = depth // chunk

    def basis_copy(k):
        part = pl.ds(k * chunk, chunk)
        return pltpu.make_async_copy(basis_hbm.at[part], basis.at[part], basis_sem.at[k])

    def tensor_copy(k):
        part = pl.ds(k * chunk, chunk)
        return pltpu.make_async_copy(tensor_hbm.at[0, part], tensor.at[part], tensor_sem.at[k])

    for k in range(count):
        basis_copy(k).start()
        tensor_copy(k).start()
    for k in range(count):
        part = slice(k * chunk, (k + 1) * chunk)
        basis_copy(k).wait()
        high, low = split(basis[part].T)
        factor[:rank, part] = high
        factor[rank:, part] = low
        tensor_copy(k).wait()
        high, low = split(tensor[part])
        first = jnp.dot(factor[:, part], high, preferred_element_type=jnp.float32)
        second = jnp.dot(factor[:rank, part], low, preferred_element_type=jnp.float32)
        term = first[:rank] + first[rank:] + second
        if k == 0:
            total[...] = term
        else:
            total[...] += term
    out[...] = total[...].reshape(nodes, rows, width)


def project(tensor, basis, nodes):
    _, depth, width = tensor.shape
    rank = basis.shape[1]
    chunk = depth // 8
    return pl.pallas_call(
        functools.partial(project_kernel, chunk),
        in_specs=[pl.BlockSpec(memory_space=pl.ANY)] * 2,
        out_specs=pl.BlockSpec(memory_space=pltpu.VMEM),
        out_shape=jax.ShapeDtypeStruct((nodes, rank // nodes, width), jnp.float32),
        scratch_shapes=[
            pltpu.VMEM((depth, rank), jnp.float32),
            pltpu.VMEM((depth, width), jnp.float32),
            pltpu.VMEM((2 * rank, depth), jnp.bfloat16),
            pltpu.VMEM((rank, width), jnp.float32),
            pltpu.SemaphoreType.DMA((8,)),
            pltpu.SemaphoreType.DMA((8,)),
        ],
        compiler_params=pltpu.CompilerParams(vmem_limit_bytes=VMEM_LIMIT),
        cost_estimate=pl.CostEstimate(
            flops=6 * rank * depth * width, bytes_accessed=4 * depth * (width + rank), transcendentals=0
        ),
        name="project",
    )(basis, tensor)


def gram_kernel(nodes, groups, cols, scale, place, *refs):
    half = nodes // 2
    share, refs = refs[0], refs[1:]
    near, near_swap, refs = refs[: half - 1], refs[half - 1 : nodes - 2], refs[nodes - 2 :]
    far, far_swap, refs = refs[0], refs[1], refs[2:]
    come, come_swap, refs = refs[:half], refs[half:nodes], refs[nodes:]
    out, left, right_high, right_low = refs
    rows, width = share.shape
    step = pl.program_id(0)
    core = place[0]

    def slot(index):
        return pl.ds(pl.multiple_of(index * rows, rows), rows)

    def columns(index, size):
        return pl.ds(pl.multiple_of(index * size, size), size)

    @pl.when(step == 0)
    def _():
        left[:rows] = share[...]
        for k in range(half - 1):
            left[slot(2 * k + 1 + core)] = near[k][...]
            left[slot(2 * k + 2 - core)] = near_swap[k][...]
        left[(nodes - 1) * rows :, columns(core, width // 2)] = far[...]
        left[(nodes - 1) * rows :, columns(1 - core, width // 2)] = far_swap[...]

    @pl.when((step == 0) & (place[2] == 1))
    def _():
        high, low = split(left[:, columns(place[1] * 2 + core, cols)])
        right_high[...] = high
        right_low[...] = low

    @pl.when((step == 0) & (place[2] != 1))
    def _():
        for k in range(half):
            high, low = split(come[k][:, columns(core, cols)])
            right_high[slot(place[3 + k])] = high
            right_low[slot(place[3 + k])] = low
            high, low = split(come_swap[k][...])
            right_high[slot(place[3 + half + k])] = high
            right_low[slot(place[3 + half + k])] = low

    size = out.shape[0]
    high, low = split(left[:, columns(step, size)].T)
    term = jnp.dot(high, right_high[...], preferred_element_type=jnp.float32)
    term += jnp.dot(low, right_high[...], preferred_element_type=jnp.float32)
    term += jnp.dot(high, right_low[...], preferred_element_type=jnp.float32)
    out[...] = term * scale


def gram_block(place, share, near, near_swap, far, far_swap, come, come_swap, nodes, groups, cols, scale):
    rows, width = share.shape
    depth = nodes * rows
    size = width // 2
    arrays = (share, *near, *near_swap, far, far_swap, *come, *come_swap)
    return pl.pallas_call(
        functools.partial(gram_kernel, nodes, groups, cols, scale),
        grid_spec=pltpu.PrefetchScalarGridSpec(
            num_scalar_prefetch=1,
            grid=(width // size,),
            in_specs=[pl.BlockSpec(x.shape, lambda s, place: (0, 0)) for x in arrays],
            out_specs=pl.BlockSpec((size, cols), lambda s, place: (s, 0)),
            scratch_shapes=[
                pltpu.VMEM((depth, width), jnp.float32),
                pltpu.VMEM((depth, cols), jnp.bfloat16),
                pltpu.VMEM((depth, cols), jnp.bfloat16),
            ],
        ),
        out_shape=jax.ShapeDtypeStruct((width, cols), jnp.float32),
        compiler_params=pltpu.CompilerParams(vmem_limit_bytes=24 * 1024 * 1024),
        cost_estimate=pl.CostEstimate(
            flops=6 * depth * width * cols, bytes_accessed=4 * width * cols, transcendentals=0
        ),
        name="gram",
    )(place, *arrays)


def gray(n):
    return n ^ (n >> 1)


def body(tensor, basis):
    nodes, feats, cores = lax.axis_size("node"), lax.axis_size("feat"), lax.axis_size("tm")
    rank = basis.shape[1]
    width = tensor.shape[2]
    groups = nodes // feats
    rows = rank // nodes
    cols = width // (groups * cores)
    scale = 1.0 / (rank * cores)
    half = nodes // 2
    node, feat, core = lax.axis_index("node"), lax.axis_index("feat"), lax.axis_index("tm")
    everyone = ("node", "feat", "tm")

    def device(n, z, c):
        return (n * feats + z) * cores + c

    def swap(x):
        return lax.ppermute(x, "tm", [(0, 1), (1, 0)])

    pieces = lax.all_to_all(project(tensor, basis, nodes), "node", 0, 0, tiled=True)
    share = lax.all_gather(jnp.sum(pieces, axis=0), "tm", axis=0, tiled=True)

    targets = (feats - 1) * groups
    table = [0] * nodes
    for idx in range(targets):
        table[gray(idx)] = idx % groups
    come = []
    for k in range(half):
        pairs = []
        for c in range(cores):
            for z in range(feats):
                for idx in range(targets):
                    source = (z * groups) ^ (k + c * half) ^ gray(idx)
                    d, g = idx // groups + 1, idx % groups
                    pairs.append((device(source, z, c), device(z * groups + g, z ^ d, c)))
        if groups == 1:
            part = share
        else:
            g = jnp.asarray(table)[node ^ (feat * groups) ^ (k + core * half)]
            part = lax.dynamic_slice_in_dim(share, g * cores * cols, cores * cols, 1)
        come.append(lax.ppermute(part, everyone, pairs))

    near = []
    for k in range(half - 1):
        pairs = [
            (device(n, z, c), device(n ^ (2 * k + 1 + c), z, c))
            for c in range(cores)
            for n in range(nodes)
            for z in range(feats)
        ]
        near.append(lax.ppermute(share, everyone, pairs))
    part = lax.dynamic_slice_in_dim(share, core * (width // 2), width // 2, 1)
    far = lax.ppermute(part, "node", [(n, n ^ (nodes - 1)) for n in range(nodes)])

    near_swap = [swap(x) for x in near]
    far_swap = swap(far)
    come_swap = [swap(lax.dynamic_slice_in_dim(x, (1 - core) * cols, cols, 1)) for x in come]

    block, g = node // groups, node % groups
    idx = ((feat ^ block) - 1) * groups + g
    base = gray(idx) ^ (block * groups) ^ node
    slots = [(k + core * half) ^ base for k in range(half)] + [(k + (1 - core) * half) ^ base for k in range(half)]
    place = jnp.stack([core, g, (block == feat).astype(jnp.int32), *slots]).astype(jnp.int32)
    return gram_block(place, share, near, near_swap, far, far_swap, come, come_swap, nodes, groups, cols, scale)


def solution(mesh):
    in_specs = (P("tm", "node", "feat"), P("node", None))
    out_specs = P("feat", ("node", "tm"))
    return jax.shard_map(body, mesh=mesh, in_specs=in_specs, out_specs=out_specs, check_vma=False)
```

time: 49.9 us -> 46.2 us (0.926)
  the two profiles are of different devices: /device:TPU:13 before, /device:TPU:0 now
where the time goes in v3:
time: 46.2 us; the launch traced here: 45.6 us
  blocking collectives  15.7 us (34%)
  starting transfers between devices  11.3 us (24%)
  Pallas kernels  11 us (24%)
  waiting for transfers between devices  7.42 us (16%)
    all_to_all x1, blocking collectives, body(): lax.all_to_all(project(tensor, basis, nodes), 'node', 0, 0, tiled=True)  13.7 us
    pallas_call x1, Pallas kernels, project(): pl.pallas_call(functools.partial(project_kernel, chunk), in_specs=[pl.Blo...  7.99 us
    ppermute x1, waiting for transfers between devices, body(): far = lax.ppermute(part, 'node', [(n, n ^ nodes - 1) for n in range(nodes)])  6.51 us
    ppermute x2, starting transfers between devices, body(): come.append(lax.ppermute(part, everyone, pairs))  6.39 us
    pallas_call x1, Pallas kernels, gram_block(): pl.pallas_call(functools.partial(gram_kernel, nodes, groups, cols, scale)...  3 us
    ppermute x1, starting transfers between devices, body(): far = lax.ppermute(part, 'node', [(n, n ^ nodes - 1) for n in range(nodes)])  2.83 us
    all_gather x1, blocking collectives, body(): share = lax.all_gather(jnp.sum(pieces, axis=0), 'tm', axis=0, tiled=True)  1.99 us
    ppermute x4, starting transfers between devices, swap(): return lax.ppermute(x, 'tm', [(0, 1), (1, 0)])  1.14 us
  transfers between devices with their start and end apart: 8, of which 4 were waited for; matrix products, arithmetic and copies ran while one was open for 0% of the time, Pallas kernels for 0%

profile of v3, /device:TPU:0, one launch (start us, length us, event | category | flops | bytes accessed | tf_op | source)
XLA Modules:
  0.0 45.6 jit_solution(6171217283319717483)
XLA Ops:
  0.0 8.0 %project.1 = f32[4,32,1024]{2,1,0:T(8,128)} custom-call(f32[4096,128]{1,0:T(8,128)} %basis_hbm.1, f32[1,4096,1024]{2,1,0:T(8,128)} %tensor_hbm.1), custom_call_target="tpu_custom_call" | custom-call | flops 3221225472 | bytes 18874368 | tf_op jit(solution)/shard_map/project/pallas_call | solution.py:57
  8.0 13.7 %all_to_all.5 = f32[4,32,1024]{2,1,0:T(8,128)S(1)} all-to-all(f32[4,32,1024]{2,1,0:T(8,128)} %project.1), channel_id=1, replica_groups=mesh['node'=4,'feat'=4,'tm'=2] {'node'}, dimensions={0} | all-to-all | bytes 1048576 | tf_op jit(solution)/shard_map/all_to_all | solution.py:177
  21.7 2.0 %all_gather.3.refs_0_ = f32[64,1024]{1,0:T(8,128)S(1)} all-gather(f32[32,1024]{1,0:T(8,128)S(1)} %reduce_sum.9), channel_id=1, replica_groups=mesh['node'=4,'feat'=4,'tm'=2] {'tm'}, dimensions={0}, use_global_device_ids=true | all-gather | bytes 393216 | tf_op jit(solution)/shard_map/all_gather | solution.py:178
  23.7 0.9 %collective-permute-start = (f32[64,1024]{1,0:T(8,128)S(1)}, f32[64,1024]{1,0:T(8,128)S(1)}, u32[]{:S(2)}, u32[]{:S(2)}) collective-permute-start(f32[64,1024]{1,0:T(8,128)S(1)} %all_gather.3.refs_0_), channel_id=1, source_target_pairs={{0,8},{2,10},{4,12},{6,14},{8,0},{10,2},{12,4},{14,6},{16,24},{18,... | collective-permute-start | bytes 786440 | tf_op jit(solution)/shard_map/ppermute | solution.py:208
  24.6 4.5 %collective-permute-start.5 = (f32[64,1024]{1,0:T(8,128)S(1)}, f32[64,1024]{1,0:T(8,128)S(1)}, u32[]{:S(2)}, u32[]{:S(2)}) collective-permute-start(f32[64,1024]{1,0:T(8,128)S(1)} %all_gather.3.refs_0_), channel_id=1, source_target_pairs={{8,2},{0,4},{16,6},{2,8},{10,14},{26,12},{28,22},{20,16},{4,18},{2... | collective-permute-start | bytes 786440 | tf_op jit(solution)/shard_map/ppermute | solution.py:198
  29.2 1.9 %collective-permute-start.4 = (f32[64,1024]{1,0:T(8,128)S(1)}, f32[64,1024]{1,0:T(8,128)S(1)}, u32[]{:S(2)}, u32[]{:S(2)}) collective-permute-start(f32[64,1024]{1,0:T(8,128)S(1)} %all_gather.3.refs_0_), channel_id=1, source_target_pairs={{0,2},{8,4},{24,6},{10,8},{2,14},{18,12},{20,22},{28,16},{12,18},{... | collective-permute-start | bytes 786440 | tf_op jit(solution)/shard_map/ppermute | solution.py:198
  31.1 2.8 %collective-permute-start.2 = (f32[64,512]{1,0:T(8,128)S(1)}, f32[64,512]{1,0:T(8,128)S(1)}, u32[]{:S(2)}, u32[]{:S(2)}) collective-permute-start(f32[64,512]{1,0:T(8,128)S(1)} %constant_dynamic-slice_fusion.2), channel_id=1, source_target_pairs={{0,24},{8,16},{16,8},{24,0},{1,25},{9,17},{17,9},{25,1},{2,26},{10... | collective-permute-start | bytes 393224 | tf_op jit(solution)/shard_map/ppermute | solution.py:210
  33.9 6.5 %collective-permute-done.2.refs_3_ = f32[64,512]{1,0:T(8,128)S(1)} collective-permute-done((f32[64,512]{1,0:T(8,128)S(1)}, f32[64,512]{1,0:T(8,128)S(1)}, u32[]{:S(2)}, u32[]{:S(2)}) %collective-permute-start.2) | collective-permute-done | bytes 131104 | tf_op jit(solution)/shard_map/ppermute | solution.py:210
  40.4 0.0 collective-permute-start.3
  40.4 0.0 collective-permute-done.refs_1_
  40.4 0.5 %collective-permute-start.1 = (f32[64,1024]{1,0:T(8,128)S(1)}, f32[64,1024]{1,0:T(8,128)S(1)}, u32[]{:S(2)}, u32[]{:S(2)}) collective-permute-start(f32[64,1024]{1,0:T(8,128)S(1)} %collective-permute-done.refs_1_), channel_id=1, source_target_pairs={{0,1},{1,0},{2,3},{3,2},{4,5},{5,4},{6,7},{7,6},{8,9},{9,8},{10,11... | collective-permute-start | bytes 786440 | tf_op jit(solution)/shard_map/ppermute | solution.py:175
  40.9 0.0 collective-permute-done.5.refs_6_
  40.9 0.1 collective-permute-start.7
  41.0 0.0 collective-permute-done.4.refs_5_
  41.1 0.5 %collective-permute-start.6 = (f32[64,512]{1,0:T(8,128)S(1)}, f32[64,512]{1,0:T(8,128)S(1)}, u32[]{:S(2)}, u32[]{:S(2)}) collective-permute-start(f32[64,512]{1,0:T(8,128)S(1)} %constant_dynamic-slice_fusion.1), channel_id=1, source_target_pairs={{0,1},{1,0},{2,3},{3,2},{4,5},{5,4},{6,7},{7,6},{8,9},{9,8},{10,11... | collective-permute-start | bytes 393224 | tf_op jit(solution)/shard_map/ppermute | solution.py:175
  41.6 0.1 stack.32.place
  41.7 0.1 collective-permute-done.3.refs_4_
  41.8 0.6 %collective-permute-done.7.refs_8_ = f32[64,512]{1,0:T(8,128)S(1)} collective-permute-done((f32[64,512]{1,0:T(8,128)S(1)}, f32[64,512]{1,0:T(8,128)S(1)}, u32[]{:S(2)}, u32[]{:S(2)}) %collective-permute-start.7) | collective-permute-done | bytes 131104 | tf_op jit(solution)/shard_map/ppermute | solution.py:175
  42.4 0.2 collective-permute-done.6.refs_7_
  42.6 0.0 collective-permute-done.1.refs_2_
  42.6 3.0 %gram.1 = f32[1024,512]{1,0:T(8,128)} custom-call(s32[7]{0:T(128)S(1)} %stack.32.place, f32[64,1024]{1,0:T(8,128)S(1)} %all_gather.3.refs_0_, f32[64,1024]{1,0:T(8,128)S(1)} %collective-permute-done.refs_1_, f32[64,1024]{1,0:T(8,128)S(1)} %collective-permute-done.1.refs_2_, f32[64,512]{1,0:T(8,128)S(1)} %collective-permute-done.2.refs_3_, ...), custom_call_target="tpu_custom_call" | custom-call | flops 805306368 | bytes 2097152 | tf_op jit(solution)/shard_map/gram/pallas_call | solution.py:133
  (4 shorter events, 0.1 us)
Async XLA Ops:
  23.7 16.7 %collective-permute-start = (f32[64,1024]{1,0:T(8,128)S(1)}, f32[64,1024]{1,0:T(8,128)S(1)}, u32[]{:S(2)}, u32[]{:S(2)}) collective-permute-start(f32[64,1024]{1,0:T(8,128)S(1)} %all_gather.3.refs_0_), channel_id=1, source_target_pairs={{0,8},{2,10},{4,12},{6,14},{8,0},{10,2},{12,4},{14,6},{16,24},{18,... | collective-permute-start | bytes 786440 | tf_op jit(solution)/shard_map/ppermute | solution.py:208
  24.6 16.3 %collective-permute-start.5 = (f32[64,1024]{1,0:T(8,128)S(1)}, f32[64,1024]{1,0:T(8,128)S(1)}, u32[]{:S(2)}, u32[]{:S(2)}) collective-permute-start(f32[64,1024]{1,0:T(8,128)S(1)} %all_gather.3.refs_0_), channel_id=1, source_target_pairs={{8,2},{0,4},{16,6},{2,8},{10,14},{26,12},{28,22},{20,16},{4,18},{2... | collective-permute-start | bytes 786440 | tf_op jit(solution)/shard_map/ppermute | solution.py:198
  29.2 11.9 %collective-permute-start.4 = (f32[64,1024]{1,0:T(8,128)S(1)}, f32[64,1024]{1,0:T(8,128)S(1)}, u32[]{:S(2)}, u32[]{:S(2)}) collective-permute-start(f32[64,1024]{1,0:T(8,128)S(1)} %all_gather.3.refs_0_), channel_id=1, source_target_pairs={{0,2},{8,4},{24,6},{10,8},{2,14},{18,12},{20,22},{28,16},{12,18},{... | collective-permute-start | bytes 786440 | tf_op jit(solution)/shard_map/ppermute | solution.py:198
  31.1 9.3 %collective-permute-start.2 = (f32[64,512]{1,0:T(8,128)S(1)}, f32[64,512]{1,0:T(8,128)S(1)}, u32[]{:S(2)}, u32[]{:S(2)}) collective-permute-start(f32[64,512]{1,0:T(8,128)S(1)} %constant_dynamic-slice_fusion.2), channel_id=1, source_target_pairs={{0,24},{8,16},{16,8},{24,0},{1,25},{9,17},{17,9},{25,1},{2,26},{10... | collective-permute-start | bytes 393224 | tf_op jit(solution)/shard_map/ppermute | solution.py:210
  40.4 1.3 %collective-permute-start.3 = (f32[64,512]{1,0:T(8,128)S(1)}, f32[64,512]{1,0:T(8,128)S(1)}, u32[]{:S(2)}, u32[]{:S(2)}) collective-permute-start(f32[64,512]{1,0:T(8,128)S(1)} %collective-permute-done.2.refs_3_), channel_id=1, source_target_pairs={{0,1},{1,0},{2,3},{3,2},{4,5},{5,4},{6,7},{7,6},{8,9},{9,8},{10,11... | collective-permute-start | bytes 393224 | tf_op jit(solution)/shard_map/ppermute | solution.py:175
  40.4 2.2 %collective-permute-start.1 = (f32[64,1024]{1,0:T(8,128)S(1)}, f32[64,1024]{1,0:T(8,128)S(1)}, u32[]{:S(2)}, u32[]{:S(2)}) collective-permute-start(f32[64,1024]{1,0:T(8,128)S(1)} %collective-permute-done.refs_1_), channel_id=1, source_target_pairs={{0,1},{1,0},{2,3},{3,2},{4,5},{5,4},{6,7},{7,6},{8,9},{9,8},{10,11... | collective-permute-start | bytes 786440 | tf_op jit(solution)/shard_map/ppermute | solution.py:175
  40.9 1.4 %collective-permute-start.7 = (f32[64,512]{1,0:T(8,128)S(1)}, f32[64,512]{1,0:T(8,128)S(1)}, u32[]{:S(2)}, u32[]{:S(2)}) collective-permute-start(f32[64,512]{1,0:T(8,128)S(1)} %constant_dynamic-slice_fusion), channel_id=1, source_target_pairs={{0,1},{1,0},{2,3},{3,2},{4,5},{5,4},{6,7},{7,6},{8,9},{9,8},{10,11... | collective-permute-start | bytes 393224 | tf_op jit(solution)/shard_map/ppermute | solution.py:175
  41.1 1.5 %collective-permute-start.6 = (f32[64,512]{1,0:T(8,128)S(1)}, f32[64,512]{1,0:T(8,128)S(1)}, u32[]{:S(2)}, u32[]{:S(2)}) collective-permute-start(f32[64,512]{1,0:T(8,128)S(1)} %constant_dynamic-slice_fusion.1), channel_id=1, source_target_pairs={{0,1},{1,0},{2,3},{3,2},{4,5},{5,4},{6,7},{7,6},{8,9},{9,8},{10,11... | collective-permute-start | bytes 393224 | tf_op jit(solution)/shard_map/ppermute | solution.py:175

commit v4 on v3

--- a/solution.py
+++ b/solution.py
@@ -7,7 +7,7 @@
 from jax.experimental.pallas import tpu as pltpu
 from jax.sharding import PartitionSpec as P
 
-VMEM_LIMIT = 56 * 1024 * 1024
+VMEM_LIMIT = 52 * 1024 * 1024
 
 
 def split(x):
@@ -15,10 +15,12 @@
     return high, (x - high.astype(jnp.float32)).astype(jnp.bfloat16)
 
 
-def project_kernel(chunk, basis_hbm, tensor_hbm, out, basis, tensor, factor, total, basis_sem, tensor_sem):
+def project_kernel(chunk, nodes, node, basis_hbm, tensor_hbm, *refs):
+    outs = refs[:nodes]
+    basis, tensor, factor, total, basis_sem, tensor_sem = refs[nodes:]
     depth, width = tensor.shape
     rank = basis.shape[1]
-    nodes, rows, _ = out.shape
+    rows = rank // nodes
     count = depth // chunk
 
     def basis_copy(k):
@@ -47,18 +49,19 @@
             total[...] = term
         else:
             total[...] += term
-    out[...] = total[...].reshape(nodes, rows, width)
-
-
-def project(tensor, basis, nodes):
+    for d in range(nodes):
+        outs[d][...] = total[pl.ds(pl.multiple_of((node[0] ^ d) * rows, rows), rows)]
+
+
+def project(tensor, basis, node, nodes):
     _, depth, width = tensor.shape
     rank = basis.shape[1]
     chunk = depth // 8
     return pl.pallas_call(
-        functools.partial(project_kernel, chunk),
-        in_specs=[pl.BlockSpec(memory_space=pl.ANY)] * 2,
-        out_specs=pl.BlockSpec(memory_space=pltpu.VMEM),
-        out_shape=jax.ShapeDtypeStruct((nodes, rank // nodes, width), jnp.float32),
+        functools.partial(project_kernel, chunk, nodes),
+        in_specs=[pl.BlockSpec(memory_space=pltpu.SMEM)] + [pl.BlockSpec(memory_space=pl.ANY)] * 2,
+        out_specs=[pl.BlockSpec(memory_space=pltpu.VMEM)] * nodes,
+        out_shape=[jax.ShapeDtypeStruct((rank // nodes, width), jnp.float32)] * nodes,
         scratch_shapes=[
             pltpu.VMEM((depth, rank), jnp.float32),
             pltpu.VMEM((depth, width), jnp.float32),
@@ -72,7 +75,7 @@
             flops=6 * rank * depth * width, bytes_accessed=4 * depth * (width + rank), transcendentals=0
         ),
         name="project",
-    )(basis, tensor)
+    )(node, basis, tensor)
 
 
 def gram_kernel(nodes, groups, cols, scale, place, *refs):
@@ -174,8 +177,11 @@
     def swap(x):
         return lax.ppermute(x, "tm", [(0, 1), (1, 0)])
 
-    pieces = lax.all_to_all(project(tensor, basis, nodes), "node", 0, 0, tiled=True)
-    share = lax.all_gather(jnp.sum(pieces, axis=0), "tm", axis=0, tiled=True)
+    pieces = project(tensor, basis, node.astype(jnp.int32).reshape(1), nodes)
+    share = pieces[0]
+    for d in range(1, nodes):
+        share += lax.ppermute(pieces[d], "node", [(n, n ^ d) for n in range(nodes)])
+    share = lax.all_gather(share, "tm", axis=0, tiled=True)
 
     targets = (feats - 1) * groups
     table = [0] * nodes

time: 46.2 us -> 43.3 us (0.937)
  blocking collectives: 15.7 us -> 1.99 us
  waiting for transfers between devices: 7.42 us -> 14 us
  starting transfers between devices: 11.3 us -> 16.1 us
  Pallas kernels: 11 us -> 10.2 us
    all_to_all x1 -> x0, blocking collectives: 13.7 us -> none  [body(): lax.all_to_all(project(tensor, basis, nodes), 'node', 0, 0, tiled=True)]
    ppermute x0 -> x3, waiting for transfers between devices: none -> 6.24 us  [body(): share += lax.ppermute(pieces[d], 'node', [(n, n ^ d) for n in range(nodes)])]
    ppermute x0 -> x3, starting transfers between devices: none -> 4.54 us  [body(): share += lax.ppermute(pieces[d], 'node', [(n, n ^ d) for n in range(nodes)])]
    pallas_call x1, Pallas kernels: 7.99 us -> 7.23 us  [project(): pl.pallas_call(functools.partial(project_kernel, chunk, nodes), in_specs=...]
  transfers between devices with their start and end apart: 8 -> 11, of which waited for: 4 -> 6; matrix products, arithmetic and copies ran while one was open for 0% -> 0% of each run, Pallas kernels for 0% -> 0%
where the time goes in v4:
time: 43.3 us; the launch traced here: 42.6 us
  starting transfers between devices  16.1 us (37%)
  waiting for transfers between devices  14 us (32%)
  Pallas kernels  10.2 us (24%)
  blocking collectives  1.99 us (5%)
    pallas_call x1, Pallas kernels, project(): pl.pallas_call(functools.partial(project_kernel, chunk, nodes), in_specs=...  7.23 us
    ppermute x1, waiting for transfers between devices, body(): far = lax.ppermute(part, 'node', [(n, n ^ nodes - 1) for n in range(nodes)])  6.84 us
    ppermute x3, waiting for transfers between devices, body(): share += lax.ppermute(pieces[d], 'node', [(n, n ^ d) for n in range(nodes)])  6.24 us
    ppermute x2, starting transfers between devices, body(): come.append(lax.ppermute(part, everyone, pairs))  6.08 us
    ppermute x3, starting transfers between devices, body(): share += lax.ppermute(pieces[d], 'node', [(n, n ^ d) for n in range(nodes)])  4.54 us
    ppermute x1, starting transfers between devices, body(): far = lax.ppermute(part, 'node', [(n, n ^ nodes - 1) for n in range(nodes)])  3.13 us
    pallas_call x1, Pallas kernels, gram_block(): pl.pallas_call(functools.partial(gram_kernel, nodes, groups, cols, scale)...  3 us
    all_gather x1, blocking collectives, body(): share = lax.all_gather(share, 'tm', axis=0, tiled=True)  1.99 us
  transfers between devices with their start and end apart: 11, of which 6 were waited for; matrix products, arithmetic and copies ran while one was open for 0% of the time, Pallas kernels for 0%

profile of v4, /device:TPU:0, one launch (start us, length us, event | category | flops | bytes accessed | tf_op | source)
XLA Modules:
  0.0 42.6 jit_solution(1611891653781136195)
XLA Ops:
  0.0 7.2 %project.1 = (f32[32,1024]{1,0:T(8,128)S(1)}, f32[32,1024]{1,0:T(8,128)S(1)}, f32[32,1024]{1,0:T(8,128)S(1)}, f32[32,1024]{1,0:T(8,128)S(1)}) custom-call(s32[1]{0:T(128)} %bitcast.6.node, f32[4096,128]{1,0:T(8,128)} %basis_hbm.1, f32[1,4096,1024]{2,1,0:T(8,128)} %tensor_hbm.1), custom_call_target="tpu_custom_call" | custom-call | flops 3221225472 | bytes 18874368 | tf_op jit(solution)/shard_map/project/pallas_call | solution.py:60
  7.2 3.0 %collective-permute-start = (f32[32,1024]{1,0:T(8,128)S(1)}, f32[32,1024]{1,0:T(8,128)S(1)}, u32[]{:S(2)}, u32[]{:S(2)}) collective-permute-start(f32[32,1024]{1,0:T(8,128)S(1)} %get-tuple-element.10), channel_id=1, source_target_pairs={{0,8},{8,0},{16,24},{24,16},{1,9},{9,1},{17,25},{25,17},{2,10},{10... | collective-permute-start | bytes 393224 | tf_op jit(solution)/shard_map/ppermute | solution.py:183
  10.2 1.5 %collective-permute-start.1 = (f32[32,1024]{1,0:T(8,128)S(1)}, f32[32,1024]{1,0:T(8,128)S(1)}, u32[]{:S(2)}, u32[]{:S(2)}) collective-permute-start(f32[32,1024]{1,0:T(8,128)S(1)} %get-tuple-element.11), channel_id=1, source_target_pairs={{0,16},{8,24},{16,0},{24,8},{1,17},{9,25},{17,1},{25,9},{2,18},{10... | collective-permute-start | bytes 393224 | tf_op jit(solution)/shard_map/ppermute | solution.py:183
  11.8 0.0 collective-permute-start.2
  11.8 2.4 %collective-permute-done = f32[32,1024]{1,0:T(8,128)S(1)} collective-permute-done((f32[32,1024]{1,0:T(8,128)S(1)}, f32[32,1024]{1,0:T(8,128)S(1)}, u32[]{:S(2)}, u32[]{:S(2)}) %collective-permute-start) | collective-permute-done | bytes 131104 | tf_op jit(solution)/shard_map/ppermute | solution.py:183
  14.1 3.9 %collective-permute-done.1 = f32[32,1024]{1,0:T(8,128)S(1)} collective-permute-done((f32[32,1024]{1,0:T(8,128)S(1)}, f32[32,1024]{1,0:T(8,128)S(1)}, u32[]{:S(2)}, u32[]{:S(2)}) %collective-permute-start.1) | collective-permute-done | bytes 131104 | tf_op jit(solution)/shard_map/ppermute | solution.py:183
  18.0 0.0 collective-permute-done.2
  18.1 2.0 %all_gather.3.refs_0_ = f32[64,1024]{1,0:T(8,128)S(1)} all-gather(f32[32,1024]{1,0:T(8,128)S(1)} %add_add_fusion), channel_id=1, replica_groups=mesh['node'=4,'feat'=4,'tm'=2] {'tm'}, dimensions={0}, use_global_device_ids=true | all-gather | bytes 393216 | tf_op jit(solution)/shard_map/all_gather | solution.py:184
  20.1 1.2 %collective-permute-start.3 = (f32[64,1024]{1,0:T(8,128)S(1)}, f32[64,1024]{1,0:T(8,128)S(1)}, u32[]{:S(2)}, u32[]{:S(2)}) collective-permute-start(f32[64,1024]{1,0:T(8,128)S(1)} %all_gather.3.refs_0_), channel_id=1, source_target_pairs={{0,8},{2,10},{4,12},{6,14},{8,0},{10,2},{12,4},{14,6},{16,24},{18,... | collective-permute-start | bytes 786440 | tf_op jit(solution)/shard_map/ppermute | solution.py:214
  21.3 4.5 %collective-permute-start.8 = (f32[64,1024]{1,0:T(8,128)S(1)}, f32[64,1024]{1,0:T(8,128)S(1)}, u32[]{:S(2)}, u32[]{:S(2)}) collective-permute-start(f32[64,1024]{1,0:T(8,128)S(1)} %all_gather.3.refs_0_), channel_id=1, source_target_pairs={{8,2},{0,4},{16,6},{2,8},{10,14},{26,12},{28,22},{20,16},{4,18},{2... | collective-permute-start | bytes 786440 | tf_op jit(solution)/shard_map/ppermute | solution.py:204
  25.8 1.6 %collective-permute-start.7 = (f32[64,1024]{1,0:T(8,128)S(1)}, f32[64,1024]{1,0:T(8,128)S(1)}, u32[]{:S(2)}, u32[]{:S(2)}) collective-permute-start(f32[64,1024]{1,0:T(8,128)S(1)} %all_gather.3.refs_0_), channel_id=1, source_target_pairs={{0,2},{8,4},{24,6},{10,8},{2,14},{18,12},{20,22},{28,16},{12,18},{... | collective-permute-start | bytes 786440 | tf_op jit(solution)/shard_map/ppermute | solution.py:204
  27.4 3.1 %collective-permute-start.5 = (f32[64,512]{1,0:T(8,128)S(1)}, f32[64,512]{1,0:T(8,128)S(1)}, u32[]{:S(2)}, u32[]{:S(2)}) collective-permute-start(f32[64,512]{1,0:T(8,128)S(1)} %constant_dynamic-slice_fusion.2), channel_id=1, source_target_pairs={{0,24},{8,16},{16,8},{24,0},{1,25},{9,17},{17,9},{25,1},{2,26},{10... | collective-permute-start | bytes 393224 | tf_op jit(solution)/shard_map/ppermute | solution.py:216
  30.5 6.8 %collective-permute-done.5.refs_3_ = f32[64,512]{1,0:T(8,128)S(1)} collective-permute-done((f32[64,512]{1,0:T(8,128)S(1)}, f32[64,512]{1,0:T(8,128)S(1)}, u32[]{:S(2)}, u32[]{:S(2)}) %collective-permute-start.5) | collective-permute-done | bytes 131104 | tf_op jit(solution)/shard_map/ppermute | solution.py:216
  37.4 0.0 collective-permute-start.6
  37.4 0.0 collective-permute-done.3.refs_1_
  37.4 0.5 %collective-permute-start.4 = (f32[64,1024]{1,0:T(8,128)S(1)}, f32[64,1024]{1,0:T(8,128)S(1)}, u32[]{:S(2)}, u32[]{:S(2)}) collective-permute-start(f32[64,1024]{1,0:T(8,128)S(1)} %collective-permute-done.3.refs_1_), channel_id=1, source_target_pairs={{0,1},{1,0},{2,3},{3,2},{4,5},{5,4},{6,7},{7,6},{8,9},{9,8},{10,11... | collective-permute-start | bytes 786440 | tf_op jit(solution)/shard_map/ppermute | solution.py:178
  37.9 0.0 collective-permute-done.8.refs_6_
  37.9 0.1 collective-permute-start.10
  38.0 0.0 collective-permute-done.7.refs_5_
  38.0 0.5 %collective-permute-start.9 = (f32[64,512]{1,0:T(8,128)S(1)}, f32[64,512]{1,0:T(8,128)S(1)}, u32[]{:S(2)}, u32[]{:S(2)}) collective-permute-start(f32[64,512]{1,0:T(8,128)S(1)} %constant_dynamic-slice_fusion.1), channel_id=1, source_target_pairs={{0,1},{1,0},{2,3},{3,2},{4,5},{5,4},{6,7},{7,6},{8,9},{9,8},{10,11... | collective-permute-start | bytes 393224 | tf_op jit(solution)/shard_map/ppermute | solution.py:178
  38.6 0.1 stack.32.place
  38.7 0.1 collective-permute-done.6.refs_4_
  38.7 0.6 %collective-permute-done.10.refs_8_ = f32[64,512]{1,0:T(8,128)S(1)} collective-permute-done((f32[64,512]{1,0:T(8,128)S(1)}, f32[64,512]{1,0:T(8,128)S(1)}, u32[]{:S(2)}, u32[]{:S(2)}) %collective-permute-start.10) | collective-permute-done | bytes 131104 | tf_op jit(solution)/shard_map/ppermute | solution.py:178
  39.3 0.2 collective-permute-done.9.refs_7_
  39.6 0.0 collective-permute-done.4.refs_2_
  39.6 3.0 %gram.1 = f32[1024,512]{1,0:T(8,128)} custom-call(s32[7]{0:T(128)S(1)} %stack.32.place, f32[64,1024]{1,0:T(8,128)S(1)} %all_gather.3.refs_0_, f32[64,1024]{1,0:T(8,128)S(1)} %collective-permute-done.3.refs_1_, f32[64,1024]{1,0:T(8,128)S(1)} %collective-permute-done.4.refs_2_, f32[64,512]{1,0:T(8,128)S(1)} %collective-permute-done.5.refs_3_, ...), custom_call_target="tpu_custom_call" | custom-call | flops 805306368 | bytes 2097152 | tf_op jit(solution)/shard_map/gram/pallas_call | solution.py:136
  (4 shorter events, 0.1 us)
Async XLA Ops:
  7.2 6.9 %collective-permute-start = (f32[32,1024]{1,0:T(8,128)S(1)}, f32[32,1024]{1,0:T(8,128)S(1)}, u32[]{:S(2)}, u32[]{:S(2)}) collective-permute-start(f32[32,1024]{1,0:T(8,128)S(1)} %get-tuple-element.10), channel_id=1, source_target_pairs={{0,8},{8,0},{16,24},{24,16},{1,9},{9,1},{17,25},{25,17},{2,10},{10... | collective-permute-start | bytes 393224 | tf_op jit(solution)/shard_map/ppermute | solution.py:183
  10.2 7.8 %collective-permute-start.1 = (f32[32,1024]{1,0:T(8,128)S(1)}, f32[32,1024]{1,0:T(8,128)S(1)}, u32[]{:S(2)}, u32[]{:S(2)}) collective-permute-start(f32[32,1024]{1,0:T(8,128)S(1)} %get-tuple-element.11), channel_id=1, source_target_pairs={{0,16},{8,24},{16,0},{24,8},{1,17},{9,25},{17,1},{25,9},{2,18},{10... | collective-permute-start | bytes 393224 | tf_op jit(solution)/shard_map/ppermute | solution.py:183
  11.8 6.3 %collective-permute-start.2 = (f32[32,1024]{1,0:T(8,128)S(1)}, f32[32,1024]{1,0:T(8,128)S(1)}, u32[]{:S(2)}, u32[]{:S(2)}) collective-permute-start(f32[32,1024]{1,0:T(8,128)S(1)} %get-tuple-element.12), channel_id=1, source_target_pairs={{0,24},{8,16},{16,8},{24,0},{1,25},{9,17},{17,9},{25,1},{2,26},{10... | collective-permute-start | bytes 393224 | tf_op jit(solution)/shard_map/ppermute | solution.py:183
  20.1 17.3 %collective-permute-start.3 = (f32[64,1024]{1,0:T(8,128)S(1)}, f32[64,1024]{1,0:T(8,128)S(1)}, u32[]{:S(2)}, u32[]{:S(2)}) collective-permute-start(f32[64,1024]{1,0:T(8,128)S(1)} %all_gather.3.refs_0_), channel_id=1, source_target_pairs={{0,8},{2,10},{4,12},{6,14},{8,0},{10,2},{12,4},{14,6},{16,24},{18,... | collective-permute-start | bytes 786440 | tf_op jit(solution)/shard_map/ppermute | solution.py:214
  21.3 16.6 %collective-permute-start.8 = (f32[64,1024]{1,0:T(8,128)S(1)}, f32[64,1024]{1,0:T(8,128)S(1)}, u32[]{:S(2)}, u32[]{:S(2)}) collective-permute-start(f32[64,1024]{1,0:T(8,128)S(1)} %all_gather.3.refs_0_), channel_id=1, source_target_pairs={{8,2},{0,4},{16,6},{2,8},{10,14},{26,12},{28,22},{20,16},{4,18},{2... | collective-permute-start | bytes 786440 | tf_op jit(solution)/shard_map/ppermute | solution.py:204
  25.8 12.2 %collective-permute-start.7 = (f32[64,1024]{1,0:T(8,128)S(1)}, f32[64,1024]{1,0:T(8,128)S(1)}, u32[]{:S(2)}, u32[]{:S(2)}) collective-permute-start(f32[64,1024]{1,0:T(8,128)S(1)} %all_gather.3.refs_0_), channel_id=1, source_target_pairs={{0,2},{8,4},{24,6},{10,8},{2,14},{18,12},{20,22},{28,16},{12,18},{... | collective-permute-start | bytes 786440 | tf_op jit(solution)/shard_map/ppermute | solution.py:204
  27.4 10.0 %collective-permute-start.5 = (f32[64,512]{1,0:T(8,128)S(1)}, f32[64,512]{1,0:T(8,128)S(1)}, u32[]{:S(2)}, u32[]{:S(2)}) collective-permute-start(f32[64,512]{1,0:T(8,128)S(1)} %constant_dynamic-slice_fusion.2), channel_id=1, source_target_pairs={{0,24},{8,16},{16,8},{24,0},{1,25},{9,17},{17,9},{25,1},{2,26},{10... | collective-permute-start | bytes 393224 | tf_op jit(solution)/shard_map/ppermute | solution.py:216
  37.4 1.3 %collective-permute-start.6 = (f32[64,512]{1,0:T(8,128)S(1)}, f32[64,512]{1,0:T(8,128)S(1)}, u32[]{:S(2)}, u32[]{:S(2)}) collective-permute-start(f32[64,512]{1,0:T(8,128)S(1)} %collective-permute-done.5.refs_3_), channel_id=1, source_target_pairs={{0,1},{1,0},{2,3},{3,2},{4,5},{5,4},{6,7},{7,6},{8,9},{9,8},{10,11... | collective-permute-start | bytes 393224 | tf_op jit(solution)/shard_map/ppermute | solution.py:178
  37.4 2.2 %collective-permute-start.4 = (f32[64,1024]{1,0:T(8,128)S(1)}, f32[64,1024]{1,0:T(8,128)S(1)}, u32[]{:S(2)}, u32[]{:S(2)}) collective-permute-start(f32[64,1024]{1,0:T(8,128)S(1)} %collective-permute-done.3.refs_1_), channel_id=1, source_target_pairs={{0,1},{1,0},{2,3},{3,2},{4,5},{5,4},{6,7},{7,6},{8,9},{9,8},{10,11... | collective-permute-start | bytes 786440 | tf_op jit(solution)/shard_map/ppermute | solution.py:178
  37.9 1.4 %collective-permute-start.10 = (f32[64,512]{1,0:T(8,128)S(1)}, f32[64,512]{1,0:T(8,128)S(1)}, u32[]{:S(2)}, u32[]{:S(2)}) collective-permute-start(f32[64,512]{1,0:T(8,128)S(1)} %constant_dynamic-slice_fusion), channel_id=1, source_target_pairs={{0,1},{1,0},{2,3},{3,2},{4,5},{5,4},{6,7},{7,6},{8,9},{9,8},{10,11... | collective-permute-start | bytes 393224 | tf_op jit(solution)/shard_map/ppermute | solution.py:178
  38.0 1.5 %collective-permute-start.9 = (f32[64,512]{1,0:T(8,128)S(1)}, f32[64,512]{1,0:T(8,128)S(1)}, u32[]{:S(2)}, u32[]{:S(2)}) collective-permute-start(f32[64,512]{1,0:T(8,128)S(1)} %constant_dynamic-slice_fusion.1), channel_id=1, source_target_pairs={{0,1},{1,0},{2,3},{3,2},{4,5},{5,4},{6,7},{7,6},{8,9},{9,8},{10,11... | collective-permute-start | bytes 393224 | tf_op jit(solution)/shard_map/ppermute | solution.py:178

commit v5 on v4

--- a/solution.py
+++ b/solution.py
@@ -84,9 +84,9 @@
     near, near_swap, refs = refs[: half - 1], refs[half - 1 : nodes - 2], refs[nodes - 2 :]
     far, far_swap, refs = refs[0], refs[1], refs[2:]
     come, come_swap, refs = refs[:half], refs[half:nodes], refs[nodes:]
-    out, left, right_high, right_low = refs
+    out_hbm, out, left, right_high, right_low, sem = refs
     rows, width = share.shape
-    step = pl.program_id(0)
+    size = min(width, 256)
     core = place[0]
 
     def slot(index):
@@ -95,22 +95,20 @@
     def columns(index, size):
         return pl.ds(pl.multiple_of(index * size, size), size)
 
-    @pl.when(step == 0)
-    def _():
-        left[:rows] = share[...]
-        for k in range(half - 1):
-            left[slot(2 * k + 1 + core)] = near[k][...]
-            left[slot(2 * k + 2 - core)] = near_swap[k][...]
-        left[(nodes - 1) * rows :, columns(core, width // 2)] = far[...]
-        left[(nodes - 1) * rows :, columns(1 - core, width // 2)] = far_swap[...]
-
-    @pl.when((step == 0) & (place[2] == 1))
+    left[:rows] = share[...]
+    for k in range(half - 1):
+        left[slot(2 * k + 1 + core)] = near[k][...]
+        left[slot(2 * k + 2 - core)] = near_swap[k][...]
+    left[(nodes - 1) * rows :, columns(core, width // 2)] = far[...]
+    left[(nodes - 1) * rows :, columns(1 - core, width // 2)] = far_swap[...]
+
+    @pl.when(place[2] == 1)
     def _():
         high, low = split(left[:, columns(place[1] * 2 + core, cols)])
         right_high[...] = high
         right_low[...] = low
 
-    @pl.when((step == 0) & (place[2] != 1))
+    @pl.when(place[2] != 1)
     def _():
         for k in range(half):
             high, low = split(come[k][:, columns(core, cols)])
@@ -120,33 +118,36 @@
             right_high[slot(place[3 + half + k])] = high
             right_low[slot(place[3 + half + k])] = low
 
-    size = out.shape[0]
-    high, low = split(left[:, columns(step, size)].T)
-    term = jnp.dot(high, right_high[...], preferred_element_type=jnp.float32)
-    term += jnp.dot(low, right_high[...], preferred_element_type=jnp.float32)
-    term += jnp.dot(high, right_low[...], preferred_element_type=jnp.float32)
-    out[...] = term * scale
+    copies = []
+    for k in range(width // size):
+        part = pl.ds(k * size, size)
+        high, low = split(left[:, k * size : (k + 1) * size].T)
+        term = jnp.dot(high, right_high[...], preferred_element_type=jnp.float32)
+        term += jnp.dot(low, right_high[...], preferred_element_type=jnp.float32)
+        term += jnp.dot(high, right_low[...], preferred_element_type=jnp.float32)
+        out[part] = term * scale
+        copies.append(pltpu.make_async_copy(out.at[part], out_hbm.at[part], sem.at[k]))
+        copies[-1].start()
+    for copy in copies:
+        copy.wait()
 
 
 def gram_block(place, share, near, near_swap, far, far_swap, come, come_swap, nodes, groups, cols, scale):
     rows, width = share.shape
     depth = nodes * rows
-    size = width // 2
     arrays = (share, *near, *near_swap, far, far_swap, *come, *come_swap)
     return pl.pallas_call(
         functools.partial(gram_kernel, nodes, groups, cols, scale),
-        grid_spec=pltpu.PrefetchScalarGridSpec(
-            num_scalar_prefetch=1,
-            grid=(width // size,),
-            in_specs=[pl.BlockSpec(x.shape, lambda s, place: (0, 0)) for x in arrays],
-            out_specs=pl.BlockSpec((size, cols), lambda s, place: (s, 0)),
-            scratch_shapes=[
-                pltpu.VMEM((depth, width), jnp.float32),
-                pltpu.VMEM((depth, cols), jnp.bfloat16),
-                pltpu.VMEM((depth, cols), jnp.bfloat16),
-            ],
-        ),
+        in_specs=[pl.BlockSpec(memory_space=pltpu.SMEM)] + [pl.BlockSpec(memory_space=pltpu.VMEM)] * len(arrays),
+        out_specs=pl.BlockSpec(memory_space=pl.ANY),
         out_shape=jax.ShapeDtypeStruct((width, cols), jnp.float32),
+        scratch_shapes=[
+            pltpu.VMEM((width, cols), jnp.float32),
+            pltpu.VMEM((depth, width), jnp.float32),
+            pltpu.VMEM((depth, cols), jnp.bfloat16),
+            pltpu.VMEM((depth, cols), jnp.bfloat16),
+            pltpu.SemaphoreType.DMA((width // min(width, 256),)),
+        ],
         compiler_params=pltpu.CompilerParams(vmem_limit_bytes=24 * 1024 * 1024),
         cost_estimate=pl.CostEstimate(
             flops=6 * depth * width * cols, bytes_accessed=4 * width * cols, transcendentals=0
@@ -181,7 +182,8 @@
     share = pieces[0]
     for d in range(1, nodes):
         share += lax.ppermute(pieces[d], "node", [(n, n ^ d) for n in range(nodes)])
-    share = lax.all_gather(share, "tm", axis=0, tiled=True)
+    both = lax.ppermute(share, "tm", [(0, 1), (1, 0)])
+    share = jnp.where(core == 0, jnp.concatenate([share, both]), jnp.concatenate([both, share]))
 
     targets = (feats - 1) * groups
     table = [0] * nodes

time: 43.3 us -> 42.4 us (0.979)
  blocking collectives: 1.99 us -> 0 us
  waiting for transfers between devices: 14 us -> 15.3 us
    all_gather x1 -> x0, blocking collectives: 1.99 us -> none  [body(): share = lax.all_gather(share, 'tm', axis=0, tiled=True)]
    ppermute x0 -> x1, waiting for transfers between devices: none -> 1.33 us  [body(): both = lax.ppermute(share, 'tm', [(0, 1), (1, 0)])]
  transfers between devices with their start and end apart: 11 -> 12, of which waited for: 6 -> 7; matrix products, arithmetic and copies ran while one was open for 0% -> 0% of each run, Pallas kernels for 0% -> 0%
where the time goes in v5:
time: 42.4 us; the launch traced here: 41.6 us
  starting transfers between devices  16.3 us (38%)
  waiting for transfers between devices  15.3 us (36%)
  Pallas kernels  9.81 us (23%)
    pallas_call x1, Pallas kernels, project(): pl.pallas_call(functools.partial(project_kernel, chunk, nodes), in_specs=...  7.23 us
    ppermute x1, waiting for transfers between devices, body(): far = lax.ppermute(part, 'node', [(n, n ^ nodes - 1) for n in range(nodes)])  6.84 us
    ppermute x3, waiting for transfers between devices, body(): share += lax.ppermute(pieces[d], 'node', [(n, n ^ d) for n in range(nodes)])  6.24 us
    ppermute x2, starting transfers between devices, body(): come.append(lax.ppermute(part, everyone, pairs))  6.08 us
    ppermute x3, starting transfers between devices, body(): share += lax.ppermute(pieces[d], 'node', [(n, n ^ d) for n in range(nodes)])  4.54 us
    ppermute x1, starting transfers between devices, body(): far = lax.ppermute(part, 'node', [(n, n ^ nodes - 1) for n in range(nodes)])  3.13 us
    pallas_call x1, Pallas kernels, gram_block(): pl.pallas_call(functools.partial(gram_kernel, nodes, groups, cols, scale)...  2.57 us
    ppermute x1, waiting for transfers between devices, body(): both = lax.ppermute(share, 'tm', [(0, 1), (1, 0)])  1.33 us
  transfers between devices with their start and end apart: 12, of which 7 were waited for; matrix products, arithmetic and copies ran while one was open for 0% of the time, Pallas kernels for 0%

profile of v5, /device:TPU:0, one launch (start us, length us, event | category | flops | bytes accessed | tf_op | source)
XLA Modules:
  0.0 41.6 jit_solution(14578173401644936947)
XLA Ops:
  0.0 7.2 %project.1 = (f32[32,1024]{1,0:T(8,128)S(1)}, f32[32,1024]{1,0:T(8,128)S(1)}, f32[32,1024]{1,0:T(8,128)S(1)}, f32[32,1024]{1,0:T(8,128)S(1)}) custom-call(s32[1]{0:T(128)} %bitcast.6.node, f32[4096,128]{1,0:T(8,128)} %basis_hbm.1, f32[1,4096,1024]{2,1,0:T(8,128)} %tensor_hbm.1), custom_call_target="tpu_custom_call" | custom-call | flops 3221225472 | bytes 18874368 | tf_op jit(solution)/shard_map/project/pallas_call | solution.py:60
  7.2 3.0 %collective-permute-start = (f32[32,1024]{1,0:T(8,128)S(1)}, f32[32,1024]{1,0:T(8,128)S(1)}, u32[]{:S(2)}, u32[]{:S(2)}) collective-permute-start(f32[32,1024]{1,0:T(8,128)S(1)} %get-tuple-element.10), channel_id=1, source_target_pairs={{0,8},{8,0},{16,24},{24,16},{1,9},{9,1},{17,25},{25,17},{2,10},{10... | collective-permute-start | bytes 393224 | tf_op jit(solution)/shard_map/ppermute | solution.py:184
  10.2 1.5 %collective-permute-start.1 = (f32[32,1024]{1,0:T(8,128)S(1)}, f32[32,1024]{1,0:T(8,128)S(1)}, u32[]{:S(2)}, u32[]{:S(2)}) collective-permute-start(f32[32,1024]{1,0:T(8,128)S(1)} %get-tuple-element.11), channel_id=1, source_target_pairs={{0,16},{8,24},{16,0},{24,8},{1,17},{9,25},{17,1},{25,9},{2,18},{10... | collective-permute-start | bytes 393224 | tf_op jit(solution)/shard_map/ppermute | solution.py:184
  11.8 0.0 collective-permute-start.2
  11.8 2.4 %collective-permute-done = f32[32,1024]{1,0:T(8,128)S(1)} collective-permute-done((f32[32,1024]{1,0:T(8,128)S(1)}, f32[32,1024]{1,0:T(8,128)S(1)}, u32[]{:S(2)}, u32[]{:S(2)}) %collective-permute-start) | collective-permute-done | bytes 131104 | tf_op jit(solution)/shard_map/ppermute | solution.py:184
  14.1 3.9 %collective-permute-done.1 = f32[32,1024]{1,0:T(8,128)S(1)} collective-permute-done((f32[32,1024]{1,0:T(8,128)S(1)}, f32[32,1024]{1,0:T(8,128)S(1)}, u32[]{:S(2)}, u32[]{:S(2)}) %collective-permute-start.1) | collective-permute-done | bytes 131104 | tf_op jit(solution)/shard_map/ppermute | solution.py:184
  18.0 0.0 collective-permute-done.2
  18.1 0.1 collective-permute-start.3
  18.1 1.3 %collective-permute-done.3 = f32[32,1024]{1,0:T(8,128)S(1)} collective-permute-done((f32[32,1024]{1,0:T(8,128)S(1)}, f32[32,1024]{1,0:T(8,128)S(1)}, u32[]{:S(2)}, u32[]{:S(2)}) %collective-permute-start.3) | collective-permute-done | bytes 131104 | tf_op jit(solution)/shard_map/ppermute | solution.py:185
  19.5 1.3 %collective-permute-start.4 = (f32[64,1024]{1,0:T(8,128)S(1)}, f32[64,1024]{1,0:T(8,128)S(1)}, u32[]{:S(2)}, u32[]{:S(2)}) collective-permute-start(f32[64,1024]{1,0:T(8,128)S(1)} %maximum_select_fusion.refs_0_), channel_id=1, source_target_pairs={{0,8},{2,10},{4,12},{6,14},{8,0},{10,2},{12,4},{14,6},{16,24},{18,... | collective-permute-start | bytes 786440 | tf_op jit(solution)/shard_map/ppermute | solution.py:216
  20.8 4.5 %collective-permute-start.9 = (f32[64,1024]{1,0:T(8,128)S(1)}, f32[64,1024]{1,0:T(8,128)S(1)}, u32[]{:S(2)}, u32[]{:S(2)}) collective-permute-start(f32[64,1024]{1,0:T(8,128)S(1)} %maximum_select_fusion.refs_0_), channel_id=1, source_target_pairs={{8,2},{0,4},{16,6},{2,8},{10,14},{26,12},{28,22},{20,16},{4,18},{2... | collective-permute-start | bytes 786440 | tf_op jit(solution)/shard_map/ppermute | solution.py:206
  25.3 1.6 %collective-permute-start.8 = (f32[64,1024]{1,0:T(8,128)S(1)}, f32[64,1024]{1,0:T(8,128)S(1)}, u32[]{:S(2)}, u32[]{:S(2)}) collective-permute-start(f32[64,1024]{1,0:T(8,128)S(1)} %maximum_select_fusion.refs_0_), channel_id=1, source_target_pairs={{0,2},{8,4},{24,6},{10,8},{2,14},{18,12},{20,22},{28,16},{12,18},{... | collective-permute-start | bytes 786440 | tf_op jit(solution)/shard_map/ppermute | solution.py:206
  26.9 3.1 %collective-permute-start.6 = (f32[64,512]{1,0:T(8,128)S(1)}, f32[64,512]{1,0:T(8,128)S(1)}, u32[]{:S(2)}, u32[]{:S(2)}) collective-permute-start(f32[64,512]{1,0:T(8,128)S(1)} %constant_dynamic-slice_fusion.2), channel_id=1, source_target_pairs={{0,24},{8,16},{16,8},{24,0},{1,25},{9,17},{17,9},{25,1},{2,26},{10... | collective-permute-start | bytes 393224 | tf_op jit(solution)/shard_map/ppermute | solution.py:218
  30.0 6.8 %collective-permute-done.6.refs_3_ = f32[64,512]{1,0:T(8,128)S(1)} collective-permute-done((f32[64,512]{1,0:T(8,128)S(1)}, f32[64,512]{1,0:T(8,128)S(1)}, u32[]{:S(2)}, u32[]{:S(2)}) %collective-permute-start.6) | collective-permute-done | bytes 131104 | tf_op jit(solution)/shard_map/ppermute | solution.py:218
  36.9 0.0 collective-permute-start.7
  36.9 0.0 collective-permute-done.4.refs_1_
  36.9 0.5 %collective-permute-start.5 = (f32[64,1024]{1,0:T(8,128)S(1)}, f32[64,1024]{1,0:T(8,128)S(1)}, u32[]{:S(2)}, u32[]{:S(2)}) collective-permute-start(f32[64,1024]{1,0:T(8,128)S(1)} %collective-permute-done.4.refs_1_), channel_id=1, source_target_pairs={{0,1},{1,0},{2,3},{3,2},{4,5},{5,4},{6,7},{7,6},{8,9},{9,8},{10,11... | collective-permute-start | bytes 786440 | tf_op jit(solution)/shard_map/ppermute | solution.py:179
  37.4 0.0 collective-permute-done.9.refs_6_
  37.4 0.1 collective-permute-start.11
  37.5 0.0 collective-permute-done.8.refs_5_
  37.5 0.5 %collective-permute-start.10 = (f32[64,512]{1,0:T(8,128)S(1)}, f32[64,512]{1,0:T(8,128)S(1)}, u32[]{:S(2)}, u32[]{:S(2)}) collective-permute-start(f32[64,512]{1,0:T(8,128)S(1)} %constant_dynamic-slice_fusion.1), channel_id=1, source_target_pairs={{0,1},{1,0},{2,3},{3,2},{4,5},{5,4},{6,7},{7,6},{8,9},{9,8},{10,11... | collective-permute-start | bytes 393224 | tf_op jit(solution)/shard_map/ppermute | solution.py:179
  38.1 0.1 stack.32.place
  38.2 0.1 collective-permute-done.7.refs_4_
  38.2 0.6 %collective-permute-done.11.refs_8_ = f32[64,512]{1,0:T(8,128)S(1)} collective-permute-done((f32[64,512]{1,0:T(8,128)S(1)}, f32[64,512]{1,0:T(8,128)S(1)}, u32[]{:S(2)}, u32[]{:S(2)}) %collective-permute-start.11) | collective-permute-done | bytes 131104 | tf_op jit(solution)/shard_map/ppermute | solution.py:179
  38.8 0.2 collective-permute-done.10.refs_7_
  39.1 0.0 collective-permute-done.5.refs_2_
  39.1 2.6 %gram.1 = f32[1024,512]{1,0:T(8,128)} custom-call(s32[7]{0:T(128)S(1)} %stack.32.place, f32[64,1024]{1,0:T(8,128)S(1)} %maximum_select_fusion.refs_0_, f32[64,1024]{1,0:T(8,128)S(1)} %collective-permute-done.4.refs_1_, f32[64,1024]{1,0:T(8,128)S(1)} %collective-permute-done.5.refs_2_, f32[64,512]{1,0:T(8,128)S(1)} %collective-permute-done.6.refs_3_, ...), custom_call_target="tpu_custom_call" | custom-call | flops 805306368 | bytes 2097152 | tf_op jit(solution)/shard_map/gram/pallas_call | solution.py:139
  (5 shorter events, 0.1 us)
Async XLA Ops:
  7.2 6.9 %collective-permute-start = (f32[32,1024]{1,0:T(8,128)S(1)}, f32[32,1024]{1,0:T(8,128)S(1)}, u32[]{:S(2)}, u32[]{:S(2)}) collective-permute-start(f32[32,1024]{1,0:T(8,128)S(1)} %get-tuple-element.10), channel_id=1, source_target_pairs={{0,8},{8,0},{16,24},{24,16},{1,9},{9,1},{17,25},{25,17},{2,10},{10... | collective-permute-start | bytes 393224 | tf_op jit(solution)/shard_map/ppermute | solution.py:184
  10.2 7.8 %collective-permute-start.1 = (f32[32,1024]{1,0:T(8,128)S(1)}, f32[32,1024]{1,0:T(8,128)S(1)}, u32[]{:S(2)}, u32[]{:S(2)}) collective-permute-start(f32[32,1024]{1,0:T(8,128)S(1)} %get-tuple-element.11), channel_id=1, source_target_pairs={{0,16},{8,24},{16,0},{24,8},{1,17},{9,25},{17,1},{25,9},{2,18},{10... | collective-permute-start | bytes 393224 | tf_op jit(solution)/shard_map/ppermute | solution.py:184
  11.8 6.3 %collective-permute-start.2 = (f32[32,1024]{1,0:T(8,128)S(1)}, f32[32,1024]{1,0:T(8,128)S(1)}, u32[]{:S(2)}, u32[]{:S(2)}) collective-permute-start(f32[32,1024]{1,0:T(8,128)S(1)} %get-tuple-element.12), channel_id=1, source_target_pairs={{0,24},{8,16},{16,8},{24,0},{1,25},{9,17},{17,9},{25,1},{2,26},{10... | collective-permute-start | bytes 393224 | tf_op jit(solution)/shard_map/ppermute | solution.py:184
  18.1 1.4 %collective-permute-start.3 = (f32[32,1024]{1,0:T(8,128)S(1)}, f32[32,1024]{1,0:T(8,128)S(1)}, u32[]{:S(2)}, u32[]{:S(2)}) collective-permute-start(f32[32,1024]{1,0:T(8,128)S(1)} %add_add_fusion), channel_id=1, source_target_pairs={{0,1},{1,0},{2,3},{3,2},{4,5},{5,4},{6,7},{7,6},{8,9},{9,8},{10,11... | collective-permute-start | bytes 393224 | tf_op jit(solution)/shard_map/ppermute | solution.py:185
  19.5 17.4 %collective-permute-start.4 = (f32[64,1024]{1,0:T(8,128)S(1)}, f32[64,1024]{1,0:T(8,128)S(1)}, u32[]{:S(2)}, u32[]{:S(2)}) collective-permute-start(f32[64,1024]{1,0:T(8,128)S(1)} %maximum_select_fusion.refs_0_), channel_id=1, source_target_pairs={{0,8},{2,10},{4,12},{6,14},{8,0},{10,2},{12,4},{14,6},{16,24},{18,... | collective-permute-start | bytes 786440 | tf_op jit(solution)/shard_map/ppermute | solution.py:216
  20.8 16.6 %collective-permute-start.9 = (f32[64,1024]{1,0:T(8,128)S(1)}, f32[64,1024]{1,0:T(8,128)S(1)}, u32[]{:S(2)}, u32[]{:S(2)}) collective-permute-start(f32[64,1024]{1,0:T(8,128)S(1)} %maximum_select_fusion.refs_0_), channel_id=1, source_target_pairs={{8,2},{0,4},{16,6},{2,8},{10,14},{26,12},{28,22},{20,16},{4,18},{2... | collective-permute-start | bytes 786440 | tf_op jit(solution)/shard_map/ppermute | solution.py:206
  25.3 12.2 %collective-permute-start.8 = (f32[64,1024]{1,0:T(8,128)S(1)}, f32[64,1024]{1,0:T(8,128)S(1)}, u32[]{:S(2)}, u32[]{:S(2)}) collective-permute-start(f32[64,1024]{1,0:T(8,128)S(1)} %maximum_select_fusion.refs_0_), channel_id=1, source_target_pairs={{0,2},{8,4},{24,6},{10,8},{2,14},{18,12},{20,22},{28,16},{12,18},{... | collective-permute-start | bytes 786440 | tf_op jit(solution)/shard_map/ppermute | solution.py:206
  26.9 10.0 %collective-permute-start.6 = (f32[64,512]{1,0:T(8,128)S(1)}, f32[64,512]{1,0:T(8,128)S(1)}, u32[]{:S(2)}, u32[]{:S(2)}) collective-permute-start(f32[64,512]{1,0:T(8,128)S(1)} %constant_dynamic-slice_fusion.2), channel_id=1, source_target_pairs={{0,24},{8,16},{16,8},{24,0},{1,25},{9,17},{17,9},{25,1},{2,26},{10... | collective-permute-start | bytes 393224 | tf_op jit(solution)/shard_map/ppermute | solution.py:218
  36.9 1.3 %collective-permute-start.7 = (f32[64,512]{1,0:T(8,128)S(1)}, f32[64,512]{1,0:T(8,128)S(1)}, u32[]{:S(2)}, u32[]{:S(2)}) collective-permute-start(f32[64,512]{1,0:T(8,128)S(1)} %collective-permute-done.6.refs_3_), channel_id=1, source_target_pairs={{0,1},{1,0},{2,3},{3,2},{4,5},{5,4},{6,7},{7,6},{8,9},{9,8},{10,11... | collective-permute-start | bytes 393224 | tf_op jit(solution)/shard_map/ppermute | solution.py:179
  36.9 2.2 %collective-permute-start.5 = (f32[64,1024]{1,0:T(8,128)S(1)}, f32[64,1024]{1,0:T(8,128)S(1)}, u32[]{:S(2)}, u32[]{:S(2)}) collective-permute-start(f32[64,1024]{1,0:T(8,128)S(1)} %collective-permute-done.4.refs_1_), channel_id=1, source_target_pairs={{0,1},{1,0},{2,3},{3,2},{4,5},{5,4},{6,7},{7,6},{8,9},{9,8},{10,11... | collective-permute-start | bytes 786440 | tf_op jit(solution)/shard_map/ppermute | solution.py:179
  37.4 1.4 %collective-permute-start.11 = (f32[64,512]{1,0:T(8,128)S(1)}, f32[64,512]{1,0:T(8,128)S(1)}, u32[]{:S(2)}, u32[]{:S(2)}) collective-permute-start(f32[64,512]{1,0:T(8,128)S(1)} %constant_dynamic-slice_fusion), channel_id=1, source_target_pairs={{0,1},{1,0},{2,3},{3,2},{4,5},{5,4},{6,7},{7,6},{8,9},{9,8},{10,11... | collective-permute-start | bytes 393224 | tf_op jit(solution)/shard_map/ppermute | solution.py:179
  37.5 1.5 %collective-permute-start.10 = (f32[64,512]{1,0:T(8,128)S(1)}, f32[64,512]{1,0:T(8,128)S(1)}, u32[]{:S(2)}, u32[]{:S(2)}) collective-permute-start(f32[64,512]{1,0:T(8,128)S(1)} %constant_dynamic-slice_fusion.1), channel_id=1, source_target_pairs={{0,1},{1,0},{2,3},{3,2},{4,5},{5,4},{6,7},{7,6},{8,9},{9,8},{10,11... | collective-permute-start | bytes 393224 | tf_op jit(solution)/shard_map/ppermute | solution.py:179

commit v6 on v5

--- a/solution.py
+++ b/solution.py
@@ -121,10 +121,11 @@
     copies = []
     for k in range(width // size):
         part = pl.ds(k * size, size)
-        high, low = split(left[:, k * size : (k + 1) * size].T)
-        term = jnp.dot(high, right_high[...], preferred_element_type=jnp.float32)
-        term += jnp.dot(low, right_high[...], preferred_element_type=jnp.float32)
-        term += jnp.dot(high, right_low[...], preferred_element_type=jnp.float32)
+        high, low = split(left[:, k * size : (k + 1) * size])
+        dims = (((0,), (0,)), ((), ()))
+        term = lax.dot_general(high, right_high[...], dims, preferred_element_type=jnp.float32)
+        term += lax.dot_general(low, right_high[...], dims, preferred_element_type=jnp.float32)
+        term += lax.dot_general(high, right_low[...], dims, preferred_element_type=jnp.float32)
         out[part] = term * scale
         copies.append(pltpu.make_async_copy(out.at[part], out_hbm.at[part], sem.at[k]))
         copies[-1].start()
@@ -195,13 +196,13 @@
         for c in range(cores):
             for z in range(feats):
                 for idx in range(targets):
-                    source = (z * groups) ^ (k + c * half) ^ gray(idx)
+                    source = (z * groups) ^ (k ^ (c * (nodes - 1))) ^ gray(idx)
                     d, g = idx // groups + 1, idx % groups
                     pairs.append((device(source, z, c), device(z * groups + g, z ^ d, c)))
         if groups == 1:
             part = share
         else:
-            g = jnp.asarray(table)[node ^ (feat * groups) ^ (k + core * half)]
+            g = jnp.asarray(table)[node ^ (feat * groups) ^ (k ^ (core * (nodes - 1)))]
             part = lax.dynamic_slice_in_dim(share, g * cores * cols, cores * cols, 1)
         come.append(lax.ppermute(part, everyone, pairs))
 
@@ -224,7 +225,7 @@
     block, g = node // groups, node % groups
     idx = ((feat ^ block) - 1) * groups + g
     base = gray(idx) ^ (block * groups) ^ node
-    slots = [(k + core * half) ^ base for k in range(half)] + [(k + (1 - core) * half) ^ base for k in range(half)]
+    slots = [(k ^ (core * (nodes - 1))) ^ base for k in range(half)] + [(k ^ ((1 - core) * (nodes - 1))) ^ base for k in range(half)]
     place = jnp.stack([core, g, (block == feat).astype(jnp.int32), *slots]).astype(jnp.int32)
     return gram_block(place, share, near, near_swap, far, far_swap, come, come_swap, nodes, groups, cols, scale)
 

time: 42.4 us -> 41.8 us (0.986); the launches traced: 41.6 us -> 41.6 us
  no operation moved by 1% of the time
where the time goes in v6:
time: 41.8 us; the launch traced here: 41.6 us
  starting transfers between devices  16.3 us (39%)
  waiting for transfers between devices  15.3 us (37%)
  Pallas kernels  9.78 us (23%)
    pallas_call x1, Pallas kernels, project(): pl.pallas_call(functools.partial(project_kernel, chunk, nodes), in_specs=...  7.23 us
    ppermute x1, waiting for transfers between devices, body(): far = lax.ppermute(part, 'node', [(n, n ^ nodes - 1) for n in range(nodes)])  6.8 us
    ppermute x3, waiting for transfers between devices, body(): share += lax.ppermute(pieces[d], 'node', [(n, n ^ d) for n in range(nodes)])  6.24 us
    ppermute x2, starting transfers between devices, body(): come.append(lax.ppermute(part, everyone, pairs))  6.08 us
    ppermute x3, starting transfers between devices, body(): share += lax.ppermute(pieces[d], 'node', [(n, n ^ d) for n in range(nodes)])  4.54 us
    ppermute x1, starting transfers between devices, body(): far = lax.ppermute(part, 'node', [(n, n ^ nodes - 1) for n in range(nodes)])  3.13 us
    pallas_call x1, Pallas kernels, gram_block(): pl.pallas_call(functools.partial(gram_kernel, nodes, groups, cols, scale)...  2.55 us
    ppermute x1, waiting for transfers between devices, body(): both = lax.ppermute(share, 'tm', [(0, 1), (1, 0)])  1.33 us
  transfers between devices with their start and end apart: 12, of which 7 were waited for; matrix products, arithmetic and copies ran while one was open for 0% of the time, Pallas kernels for 0%

profile of v6, /device:TPU:0, one launch (start us, length us, event | category | flops | bytes accessed | tf_op | source)
XLA Modules:
  0.0 41.6 jit_solution(14317216923544593557)
XLA Ops:
  0.0 7.2 %project.1 = (f32[32,1024]{1,0:T(8,128)S(1)}, f32[32,1024]{1,0:T(8,128)S(1)}, f32[32,1024]{1,0:T(8,128)S(1)}, f32[32,1024]{1,0:T(8,128)S(1)}) custom-call(s32[1]{0:T(128)} %bitcast.6.node, f32[4096,128]{1,0:T(8,128)} %basis_hbm.1, f32[1,4096,1024]{2,1,0:T(8,128)} %tensor_hbm.1), custom_call_target="tpu_custom_call" | custom-call | flops 3221225472 | bytes 18874368 | tf_op jit(solution)/shard_map/project/pallas_call | solution.py:60
  7.2 3.0 %collective-permute-start = (f32[32,1024]{1,0:T(8,128)S(1)}, f32[32,1024]{1,0:T(8,128)S(1)}, u32[]{:S(2)}, u32[]{:S(2)}) collective-permute-start(f32[32,1024]{1,0:T(8,128)S(1)} %get-tuple-element.10), channel_id=1, source_target_pairs={{0,8},{8,0},{16,24},{24,16},{1,9},{9,1},{17,25},{25,17},{2,10},{10... | collective-permute-start | bytes 393224 | tf_op jit(solution)/shard_map/ppermute | solution.py:185
  10.2 1.5 %collective-permute-start.1 = (f32[32,1024]{1,0:T(8,128)S(1)}, f32[32,1024]{1,0:T(8,128)S(1)}, u32[]{:S(2)}, u32[]{:S(2)}) collective-permute-start(f32[32,1024]{1,0:T(8,128)S(1)} %get-tuple-element.11), channel_id=1, source_target_pairs={{0,16},{8,24},{16,0},{24,8},{1,17},{9,25},{17,1},{25,9},{2,18},{10... | collective-permute-start | bytes 393224 | tf_op jit(solution)/shard_map/ppermute | solution.py:185
  11.8 0.0 collective-permute-start.2
  11.8 2.4 %collective-permute-done = f32[32,1024]{1,0:T(8,128)S(1)} collective-permute-done((f32[32,1024]{1,0:T(8,128)S(1)}, f32[32,1024]{1,0:T(8,128)S(1)}, u32[]{:S(2)}, u32[]{:S(2)}) %collective-permute-start) | collective-permute-done | bytes 131104 | tf_op jit(solution)/shard_map/ppermute | solution.py:185
  14.1 3.9 %collective-permute-done.1 = f32[32,1024]{1,0:T(8,128)S(1)} collective-permute-done((f32[32,1024]{1,0:T(8,128)S(1)}, f32[32,1024]{1,0:T(8,128)S(1)}, u32[]{:S(2)}, u32[]{:S(2)}) %collective-permute-start.1) | collective-permute-done | bytes 131104 | tf_op jit(solution)/shard_map/ppermute | solution.py:185
  18.0 0.0 collective-permute-done.2
  18.1 0.1 collective-permute-start.3
  18.1 1.3 %collective-permute-done.3 = f32[32,1024]{1,0:T(8,128)S(1)} collective-permute-done((f32[32,1024]{1,0:T(8,128)S(1)}, f32[32,1024]{1,0:T(8,128)S(1)}, u32[]{:S(2)}, u32[]{:S(2)}) %collective-permute-start.3) | collective-permute-done | bytes 131104 | tf_op jit(solution)/shard_map/ppermute | solution.py:186
  19.5 1.3 %collective-permute-start.4 = (f32[64,1024]{1,0:T(8,128)S(1)}, f32[64,1024]{1,0:T(8,128)S(1)}, u32[]{:S(2)}, u32[]{:S(2)}) collective-permute-start(f32[64,1024]{1,0:T(8,128)S(1)} %maximum_select_fusion.refs_0_), channel_id=1, source_target_pairs={{0,8},{2,10},{4,12},{6,14},{8,0},{10,2},{12,4},{14,6},{16,24},{18,... | collective-permute-start | bytes 786440 | tf_op jit(solution)/shard_map/ppermute | solution.py:217
  20.8 4.5 %collective-permute-start.9 = (f32[64,1024]{1,0:T(8,128)S(1)}, f32[64,1024]{1,0:T(8,128)S(1)}, u32[]{:S(2)}, u32[]{:S(2)}) collective-permute-start(f32[64,1024]{1,0:T(8,128)S(1)} %maximum_select_fusion.refs_0_), channel_id=1, source_target_pairs={{8,2},{0,4},{16,6},{2,8},{10,14},{26,12},{28,22},{20,16},{4,18},{2... | collective-permute-start | bytes 786440 | tf_op jit(solution)/shard_map/ppermute | solution.py:207
  25.3 1.6 %collective-permute-start.8 = (f32[64,1024]{1,0:T(8,128)S(1)}, f32[64,1024]{1,0:T(8,128)S(1)}, u32[]{:S(2)}, u32[]{:S(2)}) collective-permute-start(f32[64,1024]{1,0:T(8,128)S(1)} %maximum_select_fusion.refs_0_), channel_id=1, source_target_pairs={{0,2},{8,4},{24,6},{10,8},{2,14},{18,12},{20,22},{28,16},{12,18},{... | collective-permute-start | bytes 786440 | tf_op jit(solution)/shard_map/ppermute | solution.py:207
  26.9 3.1 %collective-permute-start.6 = (f32[64,512]{1,0:T(8,128)S(1)}, f32[64,512]{1,0:T(8,128)S(1)}, u32[]{:S(2)}, u32[]{:S(2)}) collective-permute-start(f32[64,512]{1,0:T(8,128)S(1)} %constant_dynamic-slice_fusion.2), channel_id=1, source_target_pairs={{0,24},{8,16},{16,8},{24,0},{1,25},{9,17},{17,9},{25,1},{2,26},{10... | collective-permute-start | bytes 393224 | tf_op jit(solution)/shard_map/ppermute | solution.py:219
  30.0 6.8 %collective-permute-done.6.refs_3_ = f32[64,512]{1,0:T(8,128)S(1)} collective-permute-done((f32[64,512]{1,0:T(8,128)S(1)}, f32[64,512]{1,0:T(8,128)S(1)}, u32[]{:S(2)}, u32[]{:S(2)}) %collective-permute-start.6) | collective-permute-done | bytes 131104 | tf_op jit(solution)/shard_map/ppermute | solution.py:219
  36.8 0.0 collective-permute-start.7
  36.8 0.0 collective-permute-done.4.refs_1_
  36.8 0.5 %collective-permute-start.5 = (f32[64,1024]{1,0:T(8,128)S(1)}, f32[64,1024]{1,0:T(8,128)S(1)}, u32[]{:S(2)}, u32[]{:S(2)}) collective-permute-start(f32[64,1024]{1,0:T(8,128)S(1)} %collective-permute-done.4.refs_1_), channel_id=1, source_target_pairs={{0,1},{1,0},{2,3},{3,2},{4,5},{5,4},{6,7},{7,6},{8,9},{9,8},{10,11... | collective-permute-start | bytes 786440 | tf_op jit(solution)/shard_map/ppermute | solution.py:180
  37.4 0.0 collective-permute-done.9.refs_6_
  37.4 0.1 collective-permute-start.11
  37.5 0.0 collective-permute-done.8.refs_5_
  37.5 0.5 %collective-permute-start.10 = (f32[64,512]{1,0:T(8,128)S(1)}, f32[64,512]{1,0:T(8,128)S(1)}, u32[]{:S(2)}, u32[]{:S(2)}) collective-permute-start(f32[64,512]{1,0:T(8,128)S(1)} %constant_dynamic-slice_fusion.1), channel_id=1, source_target_pairs={{0,1},{1,0},{2,3},{3,2},{4,5},{5,4},{6,7},{7,6},{8,9},{9,8},{10,11... | collective-permute-start | bytes 393224 | tf_op jit(solution)/shard_map/ppermute | solution.py:180
  38.0 0.1 stack.32.place
  38.1 0.1 collective-permute-done.7.refs_4_
  38.2 0.6 %collective-permute-done.11.refs_8_ = f32[64,512]{1,0:T(8,128)S(1)} collective-permute-done((f32[64,512]{1,0:T(8,128)S(1)}, f32[64,512]{1,0:T(8,128)S(1)}, u32[]{:S(2)}, u32[]{:S(2)}) %collective-permute-start.11) | collective-permute-done | bytes 131104 | tf_op jit(solution)/shard_map/ppermute | solution.py:180
  38.8 0.2 collective-permute-done.10.refs_7_
  39.0 0.0 collective-permute-done.5.refs_2_
  39.0 2.5 %gram.1 = f32[1024,512]{1,0:T(8,128)} custom-call(s32[7]{0:T(128)S(1)} %stack.32.place, f32[64,1024]{1,0:T(8,128)S(1)} %maximum_select_fusion.refs_0_, f32[64,1024]{1,0:T(8,128)S(1)} %collective-permute-done.4.refs_1_, f32[64,1024]{1,0:T(8,128)S(1)} %collective-permute-done.5.refs_2_, f32[64,512]{1,0:T(8,128)S(1)} %collective-permute-done.6.refs_3_, ...), custom_call_target="tpu_custom_call" | custom-call | flops 805306368 | bytes 2097152 | tf_op jit(solution)/shard_map/gram/pallas_call | solution.py:140
  (5 shorter events, 0.1 us)
Async XLA Ops:
  7.2 6.9 %collective-permute-start = (f32[32,1024]{1,0:T(8,128)S(1)}, f32[32,1024]{1,0:T(8,128)S(1)}, u32[]{:S(2)}, u32[]{:S(2)}) collective-permute-start(f32[32,1024]{1,0:T(8,128)S(1)} %get-tuple-element.10), channel_id=1, source_target_pairs={{0,8},{8,0},{16,24},{24,16},{1,9},{9,1},{17,25},{25,17},{2,10},{10... | collective-permute-start | bytes 393224 | tf_op jit(solution)/shard_map/ppermute | solution.py:185
  10.2 7.8 %collective-permute-start.1 = (f32[32,1024]{1,0:T(8,128)S(1)}, f32[32,1024]{1,0:T(8,128)S(1)}, u32[]{:S(2)}, u32[]{:S(2)}) collective-permute-start(f32[32,1024]{1,0:T(8,128)S(1)} %get-tuple-element.11), channel_id=1, source_target_pairs={{0,16},{8,24},{16,0},{24,8},{1,17},{9,25},{17,1},{25,9},{2,18},{10... | collective-permute-start | bytes 393224 | tf_op jit(solution)/shard_map/ppermute | solution.py:185
  11.8 6.3 %collective-permute-start.2 = (f32[32,1024]{1,0:T(8,128)S(1)}, f32[32,1024]{1,0:T(8,128)S(1)}, u32[]{:S(2)}, u32[]{:S(2)}) collective-permute-start(f32[32,1024]{1,0:T(8,128)S(1)} %get-tuple-element.12), channel_id=1, source_target_pairs={{0,24},{8,16},{16,8},{24,0},{1,25},{9,17},{17,9},{25,1},{2,26},{10... | collective-permute-start | bytes 393224 | tf_op jit(solution)/shard_map/ppermute | solution.py:185
  18.1 1.4 %collective-permute-start.3 = (f32[32,1024]{1,0:T(8,128)S(1)}, f32[32,1024]{1,0:T(8,128)S(1)}, u32[]{:S(2)}, u32[]{:S(2)}) collective-permute-start(f32[32,1024]{1,0:T(8,128)S(1)} %add_add_fusion), channel_id=1, source_target_pairs={{0,1},{1,0},{2,3},{3,2},{4,5},{5,4},{6,7},{7,6},{8,9},{9,8},{10,11... | collective-permute-start | bytes 393224 | tf_op jit(solution)/shard_map/ppermute | solution.py:186
  19.5 17.4 %collective-permute-start.4 = (f32[64,1024]{1,0:T(8,128)S(1)}, f32[64,1024]{1,0:T(8,128)S(1)}, u32[]{:S(2)}, u32[]{:S(2)}) collective-permute-start(f32[64,1024]{1,0:T(8,128)S(1)} %maximum_select_fusion.refs_0_), channel_id=1, source_target_pairs={{0,8},{2,10},{4,12},{6,14},{8,0},{10,2},{12,4},{14,6},{16,24},{18,... | collective-permute-start | bytes 786440 | tf_op jit(solution)/shard_map/ppermute | solution.py:217
  20.8 16.6 %collective-permute-start.9 = (f32[64,1024]{1,0:T(8,128)S(1)}, f32[64,1024]{1,0:T(8,128)S(1)}, u32[]{:S(2)}, u32[]{:S(2)}) collective-permute-start(f32[64,1024]{1,0:T(8,128)S(1)} %maximum_select_fusion.refs_0_), channel_id=1, source_target_pairs={{8,2},{0,4},{16,6},{2,8},{10,14},{26,12},{28,22},{20,16},{4,18},{2... | collective-permute-start | bytes 786440 | tf_op jit(solution)/shard_map/ppermute | solution.py:207
  25.3 12.2 %collective-permute-start.8 = (f32[64,1024]{1,0:T(8,128)S(1)}, f32[64,1024]{1,0:T(8,128)S(1)}, u32[]{:S(2)}, u32[]{:S(2)}) collective-permute-start(f32[64,1024]{1,0:T(8,128)S(1)} %maximum_select_fusion.refs_0_), channel_id=1, source_target_pairs={{0,2},{8,4},{24,6},{10,8},{2,14},{18,12},{20,22},{28,16},{12,18},{... | collective-permute-start | bytes 786440 | tf_op jit(solution)/shard_map/ppermute | solution.py:207
  26.9 9.9 %collective-permute-start.6 = (f32[64,512]{1,0:T(8,128)S(1)}, f32[64,512]{1,0:T(8,128)S(1)}, u32[]{:S(2)}, u32[]{:S(2)}) collective-permute-start(f32[64,512]{1,0:T(8,128)S(1)} %constant_dynamic-slice_fusion.2), channel_id=1, source_target_pairs={{0,24},{8,16},{16,8},{24,0},{1,25},{9,17},{17,9},{25,1},{2,26},{10... | collective-permute-start | bytes 393224 | tf_op jit(solution)/shard_map/ppermute | solution.py:219
  36.8 1.3 %collective-permute-start.7 = (f32[64,512]{1,0:T(8,128)S(1)}, f32[64,512]{1,0:T(8,128)S(1)}, u32[]{:S(2)}, u32[]{:S(2)}) collective-permute-start(f32[64,512]{1,0:T(8,128)S(1)} %collective-permute-done.6.refs_3_), channel_id=1, source_target_pairs={{0,1},{1,0},{2,3},{3,2},{4,5},{5,4},{6,7},{7,6},{8,9},{9,8},{10,11... | collective-permute-start | bytes 393224 | tf_op jit(solution)/shard_map/ppermute | solution.py:180
  36.8 2.2 %collective-permute-start.5 = (f32[64,1024]{1,0:T(8,128)S(1)}, f32[64,1024]{1,0:T(8,128)S(1)}, u32[]{:S(2)}, u32[]{:S(2)}) collective-permute-start(f32[64,1024]{1,0:T(8,128)S(1)} %collective-permute-done.4.refs_1_), channel_id=1, source_target_pairs={{0,1},{1,0},{2,3},{3,2},{4,5},{5,4},{6,7},{7,6},{8,9},{9,8},{10,11... | collective-permute-start | bytes 786440 | tf_op jit(solution)/shard_map/ppermute | solution.py:180
  37.4 1.4 %collective-permute-start.11 = (f32[64,512]{1,0:T(8,128)S(1)}, f32[64,512]{1,0:T(8,128)S(1)}, u32[]{:S(2)}, u32[]{:S(2)}) collective-permute-start(f32[64,512]{1,0:T(8,128)S(1)} %constant_dynamic-slice_fusion), channel_id=1, source_target_pairs={{0,1},{1,0},{2,3},{3,2},{4,5},{5,4},{6,7},{7,6},{8,9},{9,8},{10,11... | collective-permute-start | bytes 393224 | tf_op jit(solution)/shard_map/ppermute | solution.py:180
  37.5 1.5 %collective-permute-start.10 = (f32[64,512]{1,0:T(8,128)S(1)}, f32[64,512]{1,0:T(8,128)S(1)}, u32[]{:S(2)}, u32[]{:S(2)}) collective-permute-start(f32[64,512]{1,0:T(8,128)S(1)} %constant_dynamic-slice_fusion.1), channel_id=1, source_target_pairs={{0,1},{1,0},{2,3},{3,2},{4,5},{5,4},{6,7},{7,6},{8,9},{9,8},{10,11... | collective-permute-start | bytes 393224 | tf_op jit(solution)/shard_map/ppermute | solution.py:180

commit v7 on v6

--- a/solution.py
+++ b/solution.py
@@ -86,7 +86,7 @@
     come, come_swap, refs = refs[:half], refs[half:nodes], refs[nodes:]
     out_hbm, out, left, right_high, right_low, sem = refs
     rows, width = share.shape
-    size = min(width, 256)
+    size = min(width, 128)
     core = place[0]
 
     def slot(index):
@@ -104,17 +104,17 @@
 
     @pl.when(place[2] == 1)
     def _():
-        high, low = split(left[:, columns(place[1] * 2 + core, cols)])
+        high, low = split(left[:, columns(place[1] * 2 + core, cols)] * scale)
         right_high[...] = high
         right_low[...] = low
 
     @pl.when(place[2] != 1)
     def _():
         for k in range(half):
-            high, low = split(come[k][:, columns(core, cols)])
+            high, low = split(come[k][:, columns(core, cols)] * scale)
             right_high[slot(place[3 + k])] = high
             right_low[slot(place[3 + k])] = low
-            high, low = split(come_swap[k][...])
+            high, low = split(come_swap[k][...] * scale)
             right_high[slot(place[3 + half + k])] = high
             right_low[slot(place[3 + half + k])] = low
 
@@ -126,7 +126,7 @@
         term = lax.dot_general(high, right_high[...], dims, preferred_element_type=jnp.float32)
         term += lax.dot_general(low, right_high[...], dims, preferred_element_type=jnp.float32)
         term += lax.dot_general(high, right_low[...], dims, preferred_element_type=jnp.float32)
-        out[part] = term * scale
+        out[part] = term
         copies.append(pltpu.make_async_copy(out.at[part], out_hbm.at[part], sem.at[k]))
         copies[-1].start()
     for copy in copies:
@@ -147,7 +147,7 @@
             pltpu.VMEM((depth, width), jnp.float32),
             pltpu.VMEM((depth, cols), jnp.bfloat16),
             pltpu.VMEM((depth, cols), jnp.bfloat16),
-            pltpu.SemaphoreType.DMA((width // min(width, 256),)),
+            pltpu.SemaphoreType.DMA((width // min(width, 128),)),
         ],
         compiler_params=pltpu.CompilerParams(vmem_limit_bytes=24 * 1024 * 1024),
         cost_estimate=pl.CostEstimate(

time: 41.8 us -> 41.8 us (level)
  no operation moved by 1% of the time
where the time goes in v7:
time: 41.8 us; the launch traced here: 41.5 us
  starting transfers between devices  16.3 us (39%)
  waiting for transfers between devices  15.3 us (37%)
  Pallas kernels  9.75 us (23%)
    pallas_call x1, Pallas kernels, project(): pl.pallas_call(functools.partial(project_kernel, chunk, nodes), in_specs=...  7.23 us
    ppermute x1, waiting for transfers between devices, body(): far = lax.ppermute(part, 'node', [(n, n ^ nodes - 1) for n in range(nodes)])  6.8 us
    ppermute x3, waiting for transfers between devices, body(): share += lax.ppermute(pieces[d], 'node', [(n, n ^ d) for n in range(nodes)])  6.24 us
    ppermute x2, starting transfers between devices, body(): come.append(lax.ppermute(part, everyone, pairs))  6.08 us
    ppermute x3, starting transfers between devices, body(): share += lax.ppermute(pieces[d], 'node', [(n, n ^ d) for n in range(nodes)])  4.54 us
    ppermute x1, starting transfers between devices, body(): far = lax.ppermute(part, 'node', [(n, n ^ nodes - 1) for n in range(nodes)])  3.13 us
    pallas_call x1, Pallas kernels, gram_block(): pl.pallas_call(functools.partial(gram_kernel, nodes, groups, cols, scale)...  2.51 us
    ppermute x1, waiting for transfers between devices, body(): both = lax.ppermute(share, 'tm', [(0, 1), (1, 0)])  1.33 us
  transfers between devices with their start and end apart: 12, of which 7 were waited for; matrix products, arithmetic and copies ran while one was open for 0% of the time, Pallas kernels for 0%

profile of v7, /device:TPU:0, one launch (start us, length us, event | category | flops | bytes accessed | tf_op | source)
XLA Modules:
  0.0 41.5 jit_solution(11222505982052170043)
XLA Ops:
  0.0 7.2 %project.1 = (f32[32,1024]{1,0:T(8,128)S(1)}, f32[32,1024]{1,0:T(8,128)S(1)}, f32[32,1024]{1,0:T(8,128)S(1)}, f32[32,1024]{1,0:T(8,128)S(1)}) custom-call(s32[1]{0:T(128)} %bitcast.6.node, f32[4096,128]{1,0:T(8,128)} %basis_hbm.1, f32[1,4096,1024]{2,1,0:T(8,128)} %tensor_hbm.1), custom_call_target="tpu_custom_call" | custom-call | flops 3221225472 | bytes 18874368 | tf_op jit(solution)/shard_map/project/pallas_call | solution.py:60
  7.2 3.0 %collective-permute-start = (f32[32,1024]{1,0:T(8,128)S(1)}, f32[32,1024]{1,0:T(8,128)S(1)}, u32[]{:S(2)}, u32[]{:S(2)}) collective-permute-start(f32[32,1024]{1,0:T(8,128)S(1)} %get-tuple-element.10), channel_id=1, source_target_pairs={{0,8},{8,0},{16,24},{24,16},{1,9},{9,1},{17,25},{25,17},{2,10},{10... | collective-permute-start | bytes 393224 | tf_op jit(solution)/shard_map/ppermute | solution.py:185
  10.2 1.5 %collective-permute-start.1 = (f32[32,1024]{1,0:T(8,128)S(1)}, f32[32,1024]{1,0:T(8,128)S(1)}, u32[]{:S(2)}, u32[]{:S(2)}) collective-permute-start(f32[32,1024]{1,0:T(8,128)S(1)} %get-tuple-element.11), channel_id=1, source_target_pairs={{0,16},{8,24},{16,0},{24,8},{1,17},{9,25},{17,1},{25,9},{2,18},{10... | collective-permute-start | bytes 393224 | tf_op jit(solution)/shard_map/ppermute | solution.py:185
  11.8 0.0 collective-permute-start.2
  11.8 2.4 %collective-permute-done = f32[32,1024]{1,0:T(8,128)S(1)} collective-permute-done((f32[32,1024]{1,0:T(8,128)S(1)}, f32[32,1024]{1,0:T(8,128)S(1)}, u32[]{:S(2)}, u32[]{:S(2)}) %collective-permute-start) | collective-permute-done | bytes 131104 | tf_op jit(solution)/shard_map/ppermute | solution.py:185
  14.1 3.9 %collective-permute-done.1 = f32[32,1024]{1,0:T(8,128)S(1)} collective-permute-done((f32[32,1024]{1,0:T(8,128)S(1)}, f32[32,1024]{1,0:T(8,128)S(1)}, u32[]{:S(2)}, u32[]{:S(2)}) %collective-permute-start.1) | collective-permute-done | bytes 131104 | tf_op jit(solution)/shard_map/ppermute | solution.py:185
  18.0 0.0 collective-permute-done.2
  18.1 0.1 collective-permute-start.3
  18.1 1.3 %collective-permute-done.3 = f32[32,1024]{1,0:T(8,128)S(1)} collective-permute-done((f32[32,1024]{1,0:T(8,128)S(1)}, f32[32,1024]{1,0:T(8,128)S(1)}, u32[]{:S(2)}, u32[]{:S(2)}) %collective-permute-start.3) | collective-permute-done | bytes 131104 | tf_op jit(solution)/shard_map/ppermute | solution.py:186
  19.5 1.3 %collective-permute-start.4 = (f32[64,1024]{1,0:T(8,128)S(1)}, f32[64,1024]{1,0:T(8,128)S(1)}, u32[]{:S(2)}, u32[]{:S(2)}) collective-permute-start(f32[64,1024]{1,0:T(8,128)S(1)} %maximum_select_fusion.refs_0_), channel_id=1, source_target_pairs={{0,8},{2,10},{4,12},{6,14},{8,0},{10,2},{12,4},{14,6},{16,24},{18,... | collective-permute-start | bytes 786440 | tf_op jit(solution)/shard_map/ppermute | solution.py:217
  20.8 4.5 %collective-permute-start.9 = (f32[64,1024]{1,0:T(8,128)S(1)}, f32[64,1024]{1,0:T(8,128)S(1)}, u32[]{:S(2)}, u32[]{:S(2)}) collective-permute-start(f32[64,1024]{1,0:T(8,128)S(1)} %maximum_select_fusion.refs_0_), channel_id=1, source_target_pairs={{8,2},{0,4},{16,6},{2,8},{10,14},{26,12},{28,22},{20,16},{4,18},{2... | collective-permute-start | bytes 786440 | tf_op jit(solution)/shard_map/ppermute | solution.py:207
  25.3 1.6 %collective-permute-start.8 = (f32[64,1024]{1,0:T(8,128)S(1)}, f32[64,1024]{1,0:T(8,128)S(1)}, u32[]{:S(2)}, u32[]{:S(2)}) collective-permute-start(f32[64,1024]{1,0:T(8,128)S(1)} %maximum_select_fusion.refs_0_), channel_id=1, source_target_pairs={{0,2},{8,4},{24,6},{10,8},{2,14},{18,12},{20,22},{28,16},{12,18},{... | collective-permute-start | bytes 786440 | tf_op jit(solution)/shard_map/ppermute | solution.py:207
  26.9 3.1 %collective-permute-start.6 = (f32[64,512]{1,0:T(8,128)S(1)}, f32[64,512]{1,0:T(8,128)S(1)}, u32[]{:S(2)}, u32[]{:S(2)}) collective-permute-start(f32[64,512]{1,0:T(8,128)S(1)} %constant_dynamic-slice_fusion.2), channel_id=1, source_target_pairs={{0,24},{8,16},{16,8},{24,0},{1,25},{9,17},{17,9},{25,1},{2,26},{10... | collective-permute-start | bytes 393224 | tf_op jit(solution)/shard_map/ppermute | solution.py:219
  30.0 6.8 %collective-permute-done.6.refs_3_ = f32[64,512]{1,0:T(8,128)S(1)} collective-permute-done((f32[64,512]{1,0:T(8,128)S(1)}, f32[64,512]{1,0:T(8,128)S(1)}, u32[]{:S(2)}, u32[]{:S(2)}) %collective-permute-start.6) | collective-permute-done | bytes 131104 | tf_op jit(solution)/shard_map/ppermute | solution.py:219
  36.8 0.0 collective-permute-start.7
  36.8 0.0 collective-permute-done.4.refs_1_
  36.8 0.5 %collective-permute-start.5 = (f32[64,1024]{1,0:T(8,128)S(1)}, f32[64,1024]{1,0:T(8,128)S(1)}, u32[]{:S(2)}, u32[]{:S(2)}) collective-permute-start(f32[64,1024]{1,0:T(8,128)S(1)} %collective-permute-done.4.refs_1_), channel_id=1, source_target_pairs={{0,1},{1,0},{2,3},{3,2},{4,5},{5,4},{6,7},{7,6},{8,9},{9,8},{10,11... | collective-permute-start | bytes 786440 | tf_op jit(solution)/shard_map/ppermute | solution.py:180
  37.4 0.0 collective-permute-done.9.refs_6_
  37.4 0.1 collective-permute-start.11
  37.5 0.0 collective-permute-done.8.refs_5_
  37.5 0.5 %collective-permute-start.10 = (f32[64,512]{1,0:T(8,128)S(1)}, f32[64,512]{1,0:T(8,128)S(1)}, u32[]{:S(2)}, u32[]{:S(2)}) collective-permute-start(f32[64,512]{1,0:T(8,128)S(1)} %constant_dynamic-slice_fusion.1), channel_id=1, source_target_pairs={{0,1},{1,0},{2,3},{3,2},{4,5},{5,4},{6,7},{7,6},{8,9},{9,8},{10,11... | collective-permute-start | bytes 393224 | tf_op jit(solution)/shard_map/ppermute | solution.py:180
  38.0 0.1 stack.32.place
  38.1 0.1 collective-permute-done.7.refs_4_
  38.2 0.6 %collective-permute-done.11.refs_8_ = f32[64,512]{1,0:T(8,128)S(1)} collective-permute-done((f32[64,512]{1,0:T(8,128)S(1)}, f32[64,512]{1,0:T(8,128)S(1)}, u32[]{:S(2)}, u32[]{:S(2)}) %collective-permute-start.11) | collective-permute-done | bytes 131104 | tf_op jit(solution)/shard_map/ppermute | solution.py:180
  38.8 0.2 collective-permute-done.10.refs_7_
  39.0 0.0 collective-permute-done.5.refs_2_
  39.0 2.5 %gram.1 = f32[1024,512]{1,0:T(8,128)} custom-call(s32[7]{0:T(128)S(1)} %stack.32.place, f32[64,1024]{1,0:T(8,128)S(1)} %maximum_select_fusion.refs_0_, f32[64,1024]{1,0:T(8,128)S(1)} %collective-permute-done.4.refs_1_, f32[64,1024]{1,0:T(8,128)S(1)} %collective-permute-done.5.refs_2_, f32[64,512]{1,0:T(8,128)S(1)} %collective-permute-done.6.refs_3_, ...), custom_call_target="tpu_custom_call" | custom-call | flops 805306368 | bytes 2097152 | tf_op jit(solution)/shard_map/gram/pallas_call | solution.py:140
  (5 shorter events, 0.1 us)
Async XLA Ops:
  7.2 6.9 %collective-permute-start = (f32[32,1024]{1,0:T(8,128)S(1)}, f32[32,1024]{1,0:T(8,128)S(1)}, u32[]{:S(2)}, u32[]{:S(2)}) collective-permute-start(f32[32,1024]{1,0:T(8,128)S(1)} %get-tuple-element.10), channel_id=1, source_target_pairs={{0,8},{8,0},{16,24},{24,16},{1,9},{9,1},{17,25},{25,17},{2,10},{10... | collective-permute-start | bytes 393224 | tf_op jit(solution)/shard_map/ppermute | solution.py:185
  10.2 7.8 %collective-permute-start.1 = (f32[32,1024]{1,0:T(8,128)S(1)}, f32[32,1024]{1,0:T(8,128)S(1)}, u32[]{:S(2)}, u32[]{:S(2)}) collective-permute-start(f32[32,1024]{1,0:T(8,128)S(1)} %get-tuple-element.11), channel_id=1, source_target_pairs={{0,16},{8,24},{16,0},{24,8},{1,17},{9,25},{17,1},{25,9},{2,18},{10... | collective-permute-start | bytes 393224 | tf_op jit(solution)/shard_map/ppermute | solution.py:185
  11.8 6.3 %collective-permute-start.2 = (f32[32,1024]{1,0:T(8,128)S(1)}, f32[32,1024]{1,0:T(8,128)S(1)}, u32[]{:S(2)}, u32[]{:S(2)}) collective-permute-start(f32[32,1024]{1,0:T(8,128)S(1)} %get-tuple-element.12), channel_id=1, source_target_pairs={{0,24},{8,16},{16,8},{24,0},{1,25},{9,17},{17,9},{25,1},{2,26},{10... | collective-permute-start | bytes 393224 | tf_op jit(solution)/shard_map/ppermute | solution.py:185
  18.1 1.4 %collective-permute-start.3 = (f32[32,1024]{1,0:T(8,128)S(1)}, f32[32,1024]{1,0:T(8,128)S(1)}, u32[]{:S(2)}, u32[]{:S(2)}) collective-permute-start(f32[32,1024]{1,0:T(8,128)S(1)} %add_add_fusion), channel_id=1, source_target_pairs={{0,1},{1,0},{2,3},{3,2},{4,5},{5,4},{6,7},{7,6},{8,9},{9,8},{10,11... | collective-permute-start | bytes 393224 | tf_op jit(solution)/shard_map/ppermute | solution.py:186
  19.5 17.4 %collective-permute-start.4 = (f32[64,1024]{1,0:T(8,128)S(1)}, f32[64,1024]{1,0:T(8,128)S(1)}, u32[]{:S(2)}, u32[]{:S(2)}) collective-permute-start(f32[64,1024]{1,0:T(8,128)S(1)} %maximum_select_fusion.refs_0_), channel_id=1, source_target_pairs={{0,8},{2,10},{4,12},{6,14},{8,0},{10,2},{12,4},{14,6},{16,24},{18,... | collective-permute-start | bytes 786440 | tf_op jit(solution)/shard_map/ppermute | solution.py:217
  20.8 16.6 %collective-permute-start.9 = (f32[64,1024]{1,0:T(8,128)S(1)}, f32[64,1024]{1,0:T(8,128)S(1)}, u32[]{:S(2)}, u32[]{:S(2)}) collective-permute-start(f32[64,1024]{1,0:T(8,128)S(1)} %maximum_select_fusion.refs_0_), channel_id=1, source_target_pairs={{8,2},{0,4},{16,6},{2,8},{10,14},{26,12},{28,22},{20,16},{4,18},{2... | collective-permute-start | bytes 786440 | tf_op jit(solution)/shard_map/ppermute | solution.py:207
  25.3 12.2 %collective-permute-start.8 = (f32[64,1024]{1,0:T(8,128)S(1)}, f32[64,1024]{1,0:T(8,128)S(1)}, u32[]{:S(2)}, u32[]{:S(2)}) collective-permute-start(f32[64,1024]{1,0:T(8,128)S(1)} %maximum_select_fusion.refs_0_), channel_id=1, source_target_pairs={{0,2},{8,4},{24,6},{10,8},{2,14},{18,12},{20,22},{28,16},{12,18},{... | collective-permute-start | bytes 786440 | tf_op jit(solution)/shard_map/ppermute | solution.py:207
  26.9 9.9 %collective-permute-start.6 = (f32[64,512]{1,0:T(8,128)S(1)}, f32[64,512]{1,0:T(8,128)S(1)}, u32[]{:S(2)}, u32[]{:S(2)}) collective-permute-start(f32[64,512]{1,0:T(8,128)S(1)} %constant_dynamic-slice_fusion.2), channel_id=1, source_target_pairs={{0,24},{8,16},{16,8},{24,0},{1,25},{9,17},{17,9},{25,1},{2,26},{10... | collective-permute-start | bytes 393224 | tf_op jit(solution)/shard_map/ppermute | solution.py:219
  36.8 1.3 %collective-permute-start.7 = (f32[64,512]{1,0:T(8,128)S(1)}, f32[64,512]{1,0:T(8,128)S(1)}, u32[]{:S(2)}, u32[]{:S(2)}) collective-permute-start(f32[64,512]{1,0:T(8,128)S(1)} %collective-permute-done.6.refs_3_), channel_id=1, source_target_pairs={{0,1},{1,0},{2,3},{3,2},{4,5},{5,4},{6,7},{7,6},{8,9},{9,8},{10,11... | collective-permute-start | bytes 393224 | tf_op jit(solution)/shard_map/ppermute | solution.py:180
  36.8 2.2 %collective-permute-start.5 = (f32[64,1024]{1,0:T(8,128)S(1)}, f32[64,1024]{1,0:T(8,128)S(1)}, u32[]{:S(2)}, u32[]{:S(2)}) collective-permute-start(f32[64,1024]{1,0:T(8,128)S(1)} %collective-permute-done.4.refs_1_), channel_id=1, source_target_pairs={{0,1},{1,0},{2,3},{3,2},{4,5},{5,4},{6,7},{7,6},{8,9},{9,8},{10,11... | collective-permute-start | bytes 786440 | tf_op jit(solution)/shard_map/ppermute | solution.py:180
  37.4 1.4 %collective-permute-start.11 = (f32[64,512]{1,0:T(8,128)S(1)}, f32[64,512]{1,0:T(8,128)S(1)}, u32[]{:S(2)}, u32[]{:S(2)}) collective-permute-start(f32[64,512]{1,0:T(8,128)S(1)} %constant_dynamic-slice_fusion), channel_id=1, source_target_pairs={{0,1},{1,0},{2,3},{3,2},{4,5},{5,4},{6,7},{7,6},{8,9},{9,8},{10,11... | collective-permute-start | bytes 393224 | tf_op jit(solution)/shard_map/ppermute | solution.py:180
  37.5 1.5 %collective-permute-start.10 = (f32[64,512]{1,0:T(8,128)S(1)}, f32[64,512]{1,0:T(8,128)S(1)}, u32[]{:S(2)}, u32[]{:S(2)}) collective-permute-start(f32[64,512]{1,0:T(8,128)S(1)} %constant_dynamic-slice_fusion.1), channel_id=1, source_target_pairs={{0,1},{1,0},{2,3},{3,2},{4,5},{5,4},{6,7},{7,6},{8,9},{9,8},{10,11... | collective-permute-start | bytes 393224 | tf_op jit(solution)/shard_map/ppermute | solution.py:180
